TPU v7x, 256 devices: a whole 4x4x8 slice. The times are simulated.
256 devices in a mesh: tm: 32 (over z, x_hi, core), space: 8 (over x_lo, y).
Axes of the slice: x: 4 (x_hi: 2, x_lo: 2; x = x_hi * 2 + x_lo), y: 4, z: 8, core: 2. Of those that a mesh axis runs over, the one named last changes fastest.
Arguments:
- field: float32 [256, 256, 2048], P('tm', 'space'), may hold values from -3 to 3
- step: float32 [1], replicated, may hold values from 9.9e-05 to 0.001
- mass: float32 [1], replicated, may hold values from 0.02 to 0.05
Outputs:
- field_out: float32 [256, 256, 2048], P('tm', 'space')
All inputs are finite; a program needn't handle non-finite values.
Results may differ from a plain program's by a relative error of at most 0.0001.
Values sent between devices are 32-bit elements; how exact they have to be, the bound alone decides.
A program may use at most 64 MiB of HBM per device.

v0:
```python
import jax
import jax.numpy as jnp
from jax import lax
from jax.sharding import PartitionSpec as P

NZ = 32
ITERS = 2


HIGH = lax.Precision.HIGHEST


def with_halo(shard, sides, width, wrap):
    for axis, dim in sides:
        devices, length = (lax.axis_size(axis), shard.shape[dim])
        up = [(i, (i + 1) % devices) for i in range(devices if wrap else devices - 1)]
        down = [(j, i) for i, j in up]
        last = lax.slice_in_dim(shard, length - width, length, axis=dim)
        leading = lax.slice_in_dim(shard, 0, width, axis=dim)
        before = lax.ppermute(last, axis, up)
        after = lax.ppermute(leading, axis, down)
        shard = jnp.concatenate([before, shard, after], axis=dim)
    return shard


def local_terms(flat, depth):
    width = flat.shape[-1]
    column = lax.broadcasted_iota(jnp.int32, (width,), 0)
    zplace = column % depth
    padded = jnp.pad(flat, ((0, 0), (0, 0), (depth, depth)))
    total = padded[:, :, 2 * depth :] + padded[:, :, :width]
    upper = padded[:, :, depth + 1 : depth + 1 + width]
    lower = padded[:, :, depth - 1 : depth - 1 + width]
    total = total + jnp.where(zplace == depth - 1, 0.0, upper) + jnp.where(zplace == 0, 0.0, lower)
    return total - 8.0 * flat


def on_device(field, step, mass):
    slices = field.shape[0]
    depth = NZ
    flat = field
    total_t = slices * lax.axis_size("tm")
    wave = lax.broadcasted_iota(jnp.int32, (total_t, total_t), 0)
    times = lax.broadcasted_iota(jnp.int32, (total_t, total_t), 1)
    angle = 2.0 * jnp.pi / total_t * (wave * times % total_t).astype(jnp.float32)
    cosines = jnp.cos(angle)
    sines = jnp.sin(angle)
    freq = jnp.arange(total_t).astype(jnp.float32)
    inverse = 1.0 / (mass[0] * mass[0] + 4.0 * jnp.sin(jnp.pi * freq / total_t) ** 2)
    operator = (
        jnp.dot(cosines * inverse[None, :], cosines, precision=HIGH)
        + jnp.dot(sines * inverse[None, :], sines, precision=HIGH)
    ) / total_t
    for turn in range(ITERS):
        padded_t = with_halo(flat, (("tm", 0),), 1, True)
        padded_x = with_halo(flat, (("space", 1),), 1, False)
        lap = (
            local_terms(flat, depth)
            + padded_t[2:]
            + padded_t[:-2]
            + padded_x[:, 2:]
            + padded_x[:, :-2]
        )
        force = -lap + flat - 0.9 * flat * flat + 0.25 * flat * flat * flat
        lines = jnp.einsum(
            "ts,sab->tab",
            operator,
            lax.all_to_all(force, "tm", split_axis=1, concat_axis=0, tiled=True),
            precision=HIGH,
        )
        update = lax.all_to_all(lines, "tm", split_axis=0, concat_axis=1, tiled=True)
        flat = flat - step[0] * update
    return flat


def solution(mesh):
    return jax.shard_map(
        on_device,
        mesh=mesh,
        in_specs=(P("tm", "space", None), P(), P()),
        out_specs=P("tm", "space", None),
        check_vma=False,
    )
```

profile of v0, /device:TPU:6, one launch (start us, length us, event | category | flops | bytes accessed | tf_op | source)
XLA Modules:
  0.0 293.3 jit_solution(10033856886781438191)
XLA Ops:
  1.9 3.3 %collective-permute-start = (f32[1,32,2048]{2,0,1:T(1,128)S(1)}, f32[1,32,2048]{2,0,1:T(1,128)S(1)}, u32[]{:S(2)}, u32[]{:S(2)}) collective-permute-start(f32[1,32,2048]{2,0,1:T(1,128)S(1)} %copy.26), channel_id=1, source_target_pairs={{8,0},{16,8},{24,16},{32,24},{40,32},{48,40},{56,48},{64,56},{72,6... | collective-permute-start | bytes 786440 | tf_op jit(solution)/shard_map/ppermute | solution.py:21
  6.4 5.2 %collective-permute-start.2 = (f32[8,1,2048]{2,0,1:T(8,128)S(1)}, f32[8,1,2048]{2,0,1:T(8,128)S(1)}, u32[]{:S(2)}, u32[]{:S(2)}) collective-permute-start(f32[8,1,2048]{2,0,1:T(8,128)S(1)} %get-tuple-element.11), channel_id=1, source_target_pairs={{1,0},{2,1},{3,2},{4,3},{5,4},{6,5},{7,6},{9,8},{10,9},{11,10},{12... | collective-permute-start | bytes 196616 | tf_op jit(solution)/shard_map/ppermute | solution.py:21
  11.6 1.9 collective-permute-start.3
  13.6 6.3 %collective-permute-done.3 = f32[8,1,2048]{2,0,1:T(8,128)S(1)} collective-permute-done((f32[8,1,2048]{2,0,1:T(8,128)S(1)}, f32[8,1,2048]{2,0,1:T(8,128)S(1)}, u32[]{:S(2)}, u32[]{:S(2)}) %collective-permute-start.3) | collective-permute-done | bytes 65568 | tf_op jit(solution)/shard_map/ppermute | solution.py:20
  19.9 4.5 %fusion.1 = f32[8,32,2048]{2,0,1:T(8,128)} fusion(f32[8,32,2048]{2,0,1:T(8,128)S(1)} %copy.41, f32[8,1,2048]{2,0,1:T(8,128)S(1)} %collective-permute-done.3, f32[8,1,2048]{2,0,1:T(8,128)S(1)} %collective-permute-done.2, f32[1,32,2048]{2,0,1:T(1,128)S(1)} %collective-permute-done.1, f32[1,32,2048]{2,0,1:T(1,128)S(1)} %collective-permute-done, ...), kind=kLoop, calls=%fused_computation.7 | loop fusion | flops 12582912 | bytes 4853760 | tf_op jit(solution)/shard_map/add | solution.py:64
  24.4 11.9 %all-to-all-start = ((f32[8,32,2048]{2,0,1:T(8,128)}), f32[8,32,2048]{2,0,1:T(8,128)}, u32[]{:S(2)}, u32[]{:S(2)}) async-start(f32[8,32,2048]{2,0,1:T(8,128)} %fusion.1), calls=%async_computation | async-start | bytes 4194304 | tf_op jit(solution)/shard_map/all_to_all | solution.py:68
  39.8 46.7 %all-to-all-done = f32[8,32,2048]{2,0,1:T(8,128)} async-done(((f32[8,32,2048]{2,0,1:T(8,128)}), f32[8,32,2048]{2,0,1:T(8,128)}, u32[]{:S(2)}, u32[]{:S(2)}) %all-to-all-start) | async-done | bytes 2097184 | tf_op jit(solution)/shard_map/all_to_all | solution.py:68
  86.5 3.5 %convolution_bitcast_fusion.1 = f32[256,1,2048]{2,0,1:T(8,128)S(1)} fusion(f32[256,256]{1,0:T(8,128)S(1)} %fusion.20, f32[8,32,2048]{2,0,1:T(8,128)} %all-to-all-done), kind=kOutput, calls=%fused_computation.5 | convolution fusion | flops 1610612736 | bytes 4456448 | tf_op jit(solution)/shard_map/ts,sab->tab/dot_general | solution.py:65
  90.0 3.5 %copy.40 = f32[256,1,2048]{2,1,0:T(1,128)} copy(f32[256,1,2048]{2,0,1:T(8,128)S(1)} %convolution_bitcast_fusion.1) | data formatting | bytes 4194304 | tf_op jit(solution)/shard_map/ts,sab->tab/dot_general | solution.py:65
  93.5 6.3 %all-to-all-start.1 = ((f32[256,1,2048]{2,1,0:T(1,128)}), f32[256,1,2048]{2,1,0:T(1,128)}, u32[]{:S(2)}, u32[]{:S(2)}) async-start(f32[256,1,2048]{2,1,0:T(1,128)} %copy.40), calls=%async_computation.1 | async-start | bytes 4194304 | tf_op jit(solution)/shard_map/all_to_all | solution.py:71
  100.5 49.6 %all-to-all-done.1 = f32[256,1,2048]{2,1,0:T(1,128)} async-done(((f32[256,1,2048]{2,1,0:T(1,128)}), f32[256,1,2048]{2,1,0:T(1,128)}, u32[]{:S(2)}, u32[]{:S(2)}) %all-to-all-start.1) | async-done | bytes 2097184 | tf_op jit(solution)/shard_map/all_to_all | solution.py:71
  150.0 1.7 broadcast_multiply_fusion.1
  151.8 1.8 bitcast_subtract_fusion.1
  154.5 1.9 collective-permute-start.6
  156.4 4.1 %collective-permute-start.7 = (f32[8,1,2048]{2,0,1:T(8,128)S(1)}, f32[8,1,2048]{2,0,1:T(8,128)S(1)}, u32[]{:S(2)}, u32[]{:S(2)}) collective-permute-start(f32[8,1,2048]{2,0,1:T(8,128)S(1)} %get-tuple-element.8), channel_id=1, source_target_pairs={{0,1},{1,2},{2,3},{3,4},{4,5},{5,6},{6,7},{8,9},{9,10},{10,11},{11... | collective-permute-start | bytes 196616 | tf_op jit(solution)/shard_map/ppermute | solution.py:20
  160.6 1.5 collective-permute-done.6
  162.1 2.6 collective-permute-done.7
  164.7 3.5 %fusion.3 = f32[8,32,2048]{2,0,1:T(8,128)S(1)} fusion(f32[8,32,2048]{2,0,1:T(8,128)S(1)} %bitcast_subtract_fusion.1, f32[8,1,2048]{2,0,1:T(8,128)S(1)} %collective-permute-done.7, f32[8,1,2048]{2,0,1:T(8,128)S(1)} %collective-permute-done.6, f32[1,32,2048]{2,0,1:T(1,128)S(1)} %collective-permute-done.5, f32[1,32,2048]{2,0,1:T(1,128)S(1)} %collective-permute-done.4, ...), kind=kLoop, calls=%fused_computation.9 | loop fusion | flops 12582912 | bytes 4853760 | tf_op jit(solution)/shard_map/add | solution.py:64
  168.2 59.7 %all_to_all.48 = f32[8,32,2048]{2,0,1:T(8,128)S(1)} all-to-all(f32[8,32,2048]{2,0,1:T(8,128)S(1)} %fusion.3), channel_id=1, replica_groups=mesh['tm'=32,'space'=8] {'tm'}, dimensions={1} | all-to-all | bytes 4194304 | tf_op jit(solution)/shard_map/all_to_all | solution.py:68
  228.0 1.9 convolution_bitcast_fusion
  229.9 2.2 copy.42
  232.1 56.2 %all_to_all.49 = f32[256,1,2048]{2,1,0:T(1,128)S(1)} all-to-all(f32[256,1,2048]{2,1,0:T(1,128)S(1)} %copy.42), channel_id=1, replica_groups=mesh['tm'=32,'space'=8] {'tm'}, dimensions={0} | all-to-all | bytes 4194304 | tf_op jit(solution)/shard_map/all_to_all | solution.py:71
  288.5 2.3 bitcast_subtract_fusion
  290.8 2.5 copy.43
  (22 shorter events, 7.1 us)
Async XLA Ops:
  0.0 5.2 %copy-start = (f32[8,32,2048]{2,1,0:T(8,128)S(1)}, f32[8,32,2048]{2,1,0:T(8,128)}, u32[]{:S(2)}) copy-start(f32[8,32,2048]{2,1,0:T(8,128)} %param.3) | copy-start | bytes 6291460
  1.5 18.4 %collective-permute-start.1 = (f32[1,32,2048]{2,0,1:T(1,128)S(1)}, f32[1,32,2048]{2,0,1:T(1,128)S(1)}, u32[]{:S(2)}, u32[]{:S(2)}) collective-permute-start(f32[1,32,2048]{2,0,1:T(1,128)S(1)} %copy.28), channel_id=1, source_target_pairs={{0,8},{8,16},{16,24},{24,32},{32,40},{40,48},{48,56},{56,64},{64,7... | collective-permute-start | bytes 786440 | tf_op jit(solution)/shard_map/ppermute | solution.py:20
  1.9 18.0 %collective-permute-start = (f32[1,32,2048]{2,0,1:T(1,128)S(1)}, f32[1,32,2048]{2,0,1:T(1,128)S(1)}, u32[]{:S(2)}, u32[]{:S(2)}) collective-permute-start(f32[1,32,2048]{2,0,1:T(1,128)S(1)} %copy.26), channel_id=1, source_target_pairs={{8,0},{16,8},{24,16},{32,24},{40,32},{48,40},{56,48},{64,56},{72,6... | collective-permute-start | bytes 786440 | tf_op jit(solution)/shard_map/ppermute | solution.py:21
  6.4 7.1 %collective-permute-start.2 = (f32[8,1,2048]{2,0,1:T(8,128)S(1)}, f32[8,1,2048]{2,0,1:T(8,128)S(1)}, u32[]{:S(2)}, u32[]{:S(2)}) collective-permute-start(f32[8,1,2048]{2,0,1:T(8,128)S(1)} %get-tuple-element.11), channel_id=1, source_target_pairs={{1,0},{2,1},{3,2},{4,3},{5,4},{6,5},{7,6},{9,8},{10,9},{11,10},{12... | collective-permute-start | bytes 196616 | tf_op jit(solution)/shard_map/ppermute | solution.py:21
  11.6 8.3 %collective-permute-start.3 = (f32[8,1,2048]{2,0,1:T(8,128)S(1)}, f32[8,1,2048]{2,0,1:T(8,128)S(1)}, u32[]{:S(2)}, u32[]{:S(2)}) collective-permute-start(f32[8,1,2048]{2,0,1:T(8,128)S(1)} %get-tuple-element.12), channel_id=1, source_target_pairs={{0,1},{1,2},{2,3},{3,4},{4,5},{5,6},{6,7},{8,9},{9,10},{10,11},{11... | collective-permute-start | bytes 196616 | tf_op jit(solution)/shard_map/ppermute | solution.py:20
  24.4 62.1 %all-to-all-start = ((f32[8,32,2048]{2,0,1:T(8,128)}), f32[8,32,2048]{2,0,1:T(8,128)}, u32[]{:S(2)}, u32[]{:S(2)}) async-start(f32[8,32,2048]{2,0,1:T(8,128)} %fusion.1), calls=%async_computation | async-start | bytes 4194304 | tf_op jit(solution)/shard_map/all_to_all | solution.py:68
  93.5 56.5 %all-to-all-start.1 = ((f32[256,1,2048]{2,1,0:T(1,128)}), f32[256,1,2048]{2,1,0:T(1,128)}, u32[]{:S(2)}, u32[]{:S(2)}) async-start(f32[256,1,2048]{2,1,0:T(1,128)} %copy.40), calls=%async_computation.1 | async-start | bytes 4194304 | tf_op jit(solution)/shard_map/all_to_all | solution.py:71
  153.9 10.8 %collective-permute-start.4 = (f32[1,32,2048]{2,0,1:T(1,128)S(1)}, f32[1,32,2048]{2,0,1:T(1,128)S(1)}, u32[]{:S(2)}, u32[]{:S(2)}) collective-permute-start(f32[1,32,2048]{2,0,1:T(1,128)S(1)} %get-tuple-element.5), channel_id=1, source_target_pairs={{8,0},{16,8},{24,16},{32,24},{40,32},{48,40},{56,48},{64,56},{72,6... | collective-permute-start | bytes 786440 | tf_op jit(solution)/shard_map/ppermute | solution.py:21
  154.0 10.7 %collective-permute-start.5 = (f32[1,32,2048]{2,0,1:T(1,128)S(1)}, f32[1,32,2048]{2,0,1:T(1,128)S(1)}, u32[]{:S(2)}, u32[]{:S(2)}) collective-permute-start(f32[1,32,2048]{2,0,1:T(1,128)S(1)} %get-tuple-element.6), channel_id=1, source_target_pairs={{0,8},{8,16},{16,24},{24,32},{32,40},{40,48},{48,56},{56,64},{64,7... | collective-permute-start | bytes 786440 | tf_op jit(solution)/shard_map/ppermute | solution.py:20
  154.5 7.6 %collective-permute-start.6 = (f32[8,1,2048]{2,0,1:T(8,128)S(1)}, f32[8,1,2048]{2,0,1:T(8,128)S(1)}, u32[]{:S(2)}, u32[]{:S(2)}) collective-permute-start(f32[8,1,2048]{2,0,1:T(8,128)S(1)} %get-tuple-element.7), channel_id=1, source_target_pairs={{1,0},{2,1},{3,2},{4,3},{5,4},{6,5},{7,6},{9,8},{10,9},{11,10},{12... | collective-permute-start | bytes 196616 | tf_op jit(solution)/shard_map/ppermute | solution.py:21
  156.4 8.3 %collective-permute-start.7 = (f32[8,1,2048]{2,0,1:T(8,128)S(1)}, f32[8,1,2048]{2,0,1:T(8,128)S(1)}, u32[]{:S(2)}, u32[]{:S(2)}) collective-permute-start(f32[8,1,2048]{2,0,1:T(8,128)S(1)} %get-tuple-element.8), channel_id=1, source_target_pairs={{0,1},{1,2},{2,3},{3,4},{4,5},{5,6},{6,7},{8,9},{9,10},{10,11},{11... | collective-permute-start | bytes 196616 | tf_op jit(solution)/shard_map/ppermute | solution.py:20
where the time goes:
time: 294 us; the launch traced here: 293 us
  blocking collectives  116 us (39%)
  waiting for transfers between devices  107 us (36%)
  starting transfers between devices  35.4 us (12%)
  other arithmetic  14.2 us (5%)
  local copies, waits for them, and re-layouts  11.5 us (4%)
  matrix products  8.14 us (3%)
    all_to_all x1, blocking collectives, on_device(): lax.all_to_all(force, 'tm', split_axis=1, concat_axis=0, tiled=True)  59.7 us
    all_to_all x1, blocking collectives, on_device(): lax.all_to_all(lines, 'tm', split_axis=0, concat_axis=1, tiled=True)  56.2 us
    all_to_all x1, waiting for transfers between devices, on_device(): lax.all_to_all(lines, 'tm', split_axis=0, concat_axis=1, tiled=True)  49.6 us
    all_to_all x1, waiting for transfers between devices, on_device(): lax.all_to_all(force, 'tm', split_axis=1, concat_axis=0, tiled=True)  46.7 us
    all_to_all x1, starting transfers between devices, on_device(): lax.all_to_all(force, 'tm', split_axis=1, concat_axis=0, tiled=True)  11.9 us
    ppermute x4, starting transfers between devices, with_halo(): after = lax.ppermute(leading, axis, down)  10.5 us
    ppermute x4, waiting for transfers between devices, with_halo(): before = lax.ppermute(last, axis, up)  8.96 us
    add x2, other arithmetic, on_device(): force = -lap + flat - 0.9 * flat * flat + 0.25 * flat * flat * flat  8.06 us
  transfers between devices with their start and end apart: 10, of which 5 were waited for; matrix products, arithmetic and copies ran while one was open for 1% of the time, Pallas kernels for 0%

commit v1 on v0

v1 whole, which is shorter than its diff:
```python
import jax
import jax.numpy as jnp
from jax import lax
from jax.sharding import PartitionSpec as P

NZ = 32
ITERS = 2
HIGH = lax.Precision.HIGHEST


def x_neighbours(shard, axis):
    devices = lax.axis_size(axis)
    up = [(i, i + 1) for i in range(devices - 1)]
    down = [(j, i) for i, j in up]
    before = lax.ppermute(shard[:, -1:], axis, up)
    after = lax.ppermute(shard[:, :1], axis, down)
    padded = jnp.concatenate([before, shard, after], axis=1)
    return padded[:, 2:] + padded[:, :-2]


def plane_neighbours(flat, depth):
    width = flat.shape[-1]
    zplace = lax.broadcasted_iota(jnp.int32, (width,), 0) % depth
    padded = jnp.pad(flat, ((0, 0), (0, 0), (depth, depth)))
    total = padded[:, :, 2 * depth :] + padded[:, :, :width]
    upper = padded[:, :, depth + 1 : depth + 1 + width]
    lower = padded[:, :, depth - 1 : depth - 1 + width]
    return total + jnp.where(zplace == depth - 1, 0.0, upper) + jnp.where(zplace == 0, 0.0, lower)


def on_device(field, step, mass):
    slices = field.shape[0]
    blocks = lax.axis_size("tm")
    m = mass[0]
    theta = 2.0 * jnp.arcsinh(0.5 * m)
    kappa = 0.5 / jnp.sinh(theta)
    place = jnp.arange(slices)
    power = lambda k: jnp.exp(-theta * k.astype(jnp.float32))
    moments = jnp.stack([power(slices - 1 - place), power(place)])
    rows = jnp.arange(blocks)
    lag = (rows[:, None] - rows[None, :] - 1) % blocks
    whole = -jnp.expm1(-theta * (slices * blocks))
    left = power(slices * lag) / whole
    mix = jnp.zeros((blocks, 2, blocks, 2), jnp.float32)
    mix = mix.at[:, 0, :, 0].set(left).at[:, 1, :, 1].set(left.T).reshape(2 * blocks, 2 * blocks)
    inner = kappa * power(jnp.abs(place[:, None] - place[None, :]))
    edges = kappa * jnp.stack([power(place + 1), power(slices - place)], axis=1)
    flat = field
    for turn in range(ITERS):
        near = x_neighbours(flat, "space") + plane_neighbours(flat, NZ)
        g = flat * ((7.0 - m * m) + flat * (0.25 * flat - 0.9)) - near
        own = jnp.einsum("ms,sab->mab", moments, g, precision=HIGH)
        every = lax.all_to_all(own, "tm", split_axis=1, concat_axis=0, tiled=True)
        mixed = jnp.einsum("pq,qab->pab", mix, every, precision=HIGH)
        ends = lax.all_to_all(mixed, "tm", split_axis=0, concat_axis=1, tiled=True)
        solved = jnp.einsum("ts,sab->tab", inner, g, precision=HIGH)
        solved = solved + jnp.einsum("tm,mab->tab", edges, ends, precision=HIGH)
        flat = flat - step[0] * (flat + solved)
    return flat


def solution(mesh):
    return jax.shard_map(
        on_device,
        mesh=mesh,
        in_specs=(P("tm", "space", None), P(), P()),
        out_specs=P("tm", "space", None),
        check_vma=False,
    )
```

time: 294 us -> 163 us (0.55)
  blocking collectives: 116 us -> 22.5 us
  waiting for transfers between devices: 107 us -> 52.9 us
  matrix products: 8.14 us -> 22.7 us
    all_to_all x2 -> x1, blocking collectives: 116 us -> 22.5 us  [on_device(): every = lax.all_to_all(own, 'tm', split_axis=1, concat_axis=0, tiled=True)]
    all_to_all x2 -> x3, waiting for transfers between devices: 96.3 us -> 43.1 us  [the longest x2 26.6 us: on_device(): ends = lax.all_to_all(mixed, 'tm', split_axis=0, concat_axis=1, tiled=True)]
    dot_general x4 -> x8, matrix products: 8.14 us -> 22.7 us  [the longest x2 9.32 us: on_device(): solved = solved + jnp.einsum('tm,mab->tab', edges, ends, precision=HIGH)]
    add x2 -> x0, other arithmetic: 8.06 us -> none  [on_device(): force = -lap + flat - 0.9 * flat * flat + 0.25 * flat * flat * flat]
    sub x2, other arithmetic: 4.1 us -> 11 us  [on_device(): g = flat * (7.0 - m * m + flat * (0.25 * flat - 0.9)) - near]
    unnamed x3 -> x5, local copies, waits for them, and re-layouts: 1.22 us -> 5.44 us
    ppermute x8 -> x4, starting transfers between devices: 17.1 us -> 13 us  [the longest x2 7.11 us: x_neighbours(): after = lax.ppermute(shard[:, :1], axis, down)]
    all_to_all x2 -> x3, starting transfers between devices: 18.2 us -> 21.6 us  [the longest x1 11.6 us: on_device(): every = lax.all_to_all(own, 'tm', split_axis=1, concat_axis=0, tiled=True)]
  transfers between devices with their start and end apart: 10 -> 7, of which waited for: 5 -> 6; matrix products, arithmetic and copies ran while one was open for 1% -> 6% of each run, Pallas kernels for 0% -> 0%
where the time goes in v1:
time: 163 us; the launch traced here: 162 us
  waiting for transfers between devices  52.9 us (32%)
  starting transfers between devices  34.6 us (21%)
  matrix products  22.7 us (14%)
  blocking collectives  22.5 us (14%)
  local copies, waits for them, and re-layouts  14.1 us (9%)
  other arithmetic  13.5 us (8%)
  between operations  1.96 us (1%)
    all_to_all x2, waiting for transfers between devices, on_device(): ends = lax.all_to_all(mixed, 'tm', split_axis=0, concat_axis=1, tiled=True)  26.6 us
    all_to_all x1, blocking collectives, on_device(): every = lax.all_to_all(own, 'tm', split_axis=1, concat_axis=0, tiled=True)  22.5 us
    all_to_all x1, waiting for transfers between devices, on_device(): every = lax.all_to_all(own, 'tm', split_axis=1, concat_axis=0, tiled=True)  16.5 us
    all_to_all x1, starting transfers between devices, on_device(): every = lax.all_to_all(own, 'tm', split_axis=1, concat_axis=0, tiled=True)  11.6 us
    sub x2, other arithmetic, on_device(): g = flat * (7.0 - m * m + flat * (0.25 * flat - 0.9)) - near  11 us
    all_to_all x2, starting transfers between devices, on_device(): ends = lax.all_to_all(mixed, 'tm', split_axis=0, concat_axis=1, tiled=True)  9.99 us
    ppermute x2, waiting for transfers between devices, x_neighbours(): before = lax.ppermute(shard[:, -1:], axis, up)  9.5 us
    dot_general x2, matrix products, on_device(): solved = solved + jnp.einsum('tm,mab->tab', edges, ends, precision=HIGH)  9.32 us
  transfers between devices with their start and end apart: 7, of which 6 were waited for; matrix products, arithmetic and copies ran while one was open for 6% of the time, Pallas kernels for 0%

profile of v1, /device:TPU:6, one launch (start us, length us, event | category | flops | bytes accessed | tf_op | source)
XLA Modules:
  0.0 162.3 jit_solution(8040271749777704107)
XLA Ops:
  0.0 2.8 %copy.50 = f32[8,32,2048]{2,0,1:T(8,128)S(1)} copy(f32[8,32,2048]{2,1,0:T(8,128)} %param.7) | data formatting | bytes 4194304 | tf_op args[0]
  4.1 5.2 %collective-permute-start = (f32[8,1,2048]{2,0,1:T(8,128)S(1)}, f32[8,1,2048]{2,0,1:T(8,128)S(1)}, u32[]{:S(2)}, u32[]{:S(2)}) collective-permute-start(f32[8,1,2048]{2,0,1:T(8,128)S(1)} %get-tuple-element.31), channel_id=1, source_target_pairs={{1,0},{2,1},{3,2},{4,3},{5,4},{6,5},{7,6},{9,8},{10,9},{11,10},{12... | collective-permute-start | bytes 196616 | tf_op jit(solution)/shard_map/ppermute | solution.py:16
  9.3 1.9 %collective-permute-start.1 = (f32[8,1,2048]{2,0,1:T(8,128)S(1)}, f32[8,1,2048]{2,0,1:T(8,128)S(1)}, u32[]{:S(2)}, u32[]{:S(2)}) collective-permute-start(f32[8,1,2048]{2,0,1:T(8,128)S(1)} %get-tuple-element.32), channel_id=1, source_target_pairs={{0,1},{1,2},{2,3},{3,4},{4,5},{5,6},{6,7},{8,9},{9,10},{10,11},{11... | collective-permute-start | bytes 196616 | tf_op jit(solution)/shard_map/ppermute | solution.py:15
  12.1 5.5 %collective-permute-done.1 = f32[8,1,2048]{2,0,1:T(8,128)S(1)} collective-permute-done((f32[8,1,2048]{2,0,1:T(8,128)S(1)}, f32[8,1,2048]{2,0,1:T(8,128)S(1)}, u32[]{:S(2)}, u32[]{:S(2)}) %collective-permute-start.1) | collective-permute-done | bytes 65568 | tf_op jit(solution)/shard_map/ppermute | solution.py:15
  17.6 8.5 %fusion.11 = f32[8,32,2048]{2,0,1:T(8,128)S(1)} fusion(f32[8,32,2048]{2,0,1:T(8,128)} %copy-done.1, f32[8,1,2048]{2,0,1:T(8,128)S(1)} %collective-permute-done.1, f32[8,1,2048]{2,0,1:T(8,128)S(1)} %collective-permute-done, f32[]{:T(128)} %bitcast.5, pred[2048]{0:T(1024)(128)(4,1)S(1)} %get-tuple-element.33, pred[2048]{0:T(1024)(128)(4,1)S(1)} %get-tuple-element.34), kind=kLoop, calls=%fused_computation.18 | loop fusion | flops 7864320 | bytes 4329476 | tf_op jit(solution)/shard_map/sub | solution.py:51
  26.2 2.6 %fusion.44 = f32[2,32,2048]{2,0,1:T(2,128)} fusion(f32[8,32,2048]{2,0,1:T(8,128)S(1)} %fusion.11, f32[1,8]{1,0:T(1,128)S(1)} %get-tuple-element.35, f32[1,8]{1,0:T(1,128)S(1)} %get-tuple-element.36), kind=kOutput, calls=%fused_computation.71 | convolution fusion | flops 12582928 | bytes 2621504 | tf_op jit(solution)/shard_map/ms,sab->mab/dot_general | solution.py:52
  28.8 11.6 %all-to-all-start = ((f32[2,32,2048]{2,0,1:T(2,128)}), f32[2,32,2048]{2,0,1:T(2,128)}, u32[]{:S(2)}, u32[]{:S(2)}) async-start(f32[2,32,2048]{2,0,1:T(2,128)} %fusion.44), calls=%async_computation | async-start | bytes 1048576 | tf_op jit(solution)/shard_map/all_to_all | solution.py:53
  41.6 16.5 %all-to-all-done = f32[2,32,2048]{2,0,1:T(2,128)} async-done(((f32[2,32,2048]{2,0,1:T(2,128)}), f32[2,32,2048]{2,0,1:T(2,128)}, u32[]{:S(2)}, u32[]{:S(2)}) %all-to-all-start) | async-done | bytes 524320 | tf_op jit(solution)/shard_map/all_to_all | solution.py:53
  58.1 1.4 reshape.242
  61.4 5.0 %all-to-all-start.1 = ((f32[64,1,2048]{2,1,0:T(1,128)}), f32[64,1,2048]{2,1,0:T(1,128)S(1)}, u32[]{:S(2)}, u32[]{:S(2)}) async-start(f32[64,1,2048]{2,1,0:T(1,128)} %copy.48), calls=%async_computation.1 | async-start | bytes 1048576 | tf_op jit(solution)/shard_map/all_to_all | solution.py:55
  67.3 3.1 %fusion.36 = f32[8,32,2048]{2,0,1:T(8,128)} fusion(f32[8,32,2048]{2,0,1:T(8,128)S(1)} %fusion.11, f32[]{:T(128)S(6)} %neg.4, f32[]{:T(128)S(6)} %div.22), kind=kOutput, calls=%fused_computation.56 | convolution fusion | flops 50331968 | bytes 4194312 | tf_op jit(solution)/shard_map/ts,sab->tab/dot_general | solution.py:56
  70.5 13.7 %all-to-all-done.1 = f32[64,1,2048]{2,1,0:T(1,128)S(1)} async-done(((f32[64,1,2048]{2,1,0:T(1,128)}), f32[64,1,2048]{2,1,0:T(1,128)S(1)}, u32[]{:S(2)}, u32[]{:S(2)}) %all-to-all-start.1) | async-done | bytes 524320 | tf_op jit(solution)/shard_map/all_to_all | solution.py:55
  85.7 5.3 %fusion.5 = f32[8,32,2048]{2,0,1:T(8,128)S(1)} fusion(f32[8,32,2048]{2,0,1:T(8,128)} %fusion.36, f32[]{:T(128)} %bitcast.52, f32[32,2,1,2048]{3,1,0,2:T(2,128)S(1)} %all_to_all.52, f32[8,1]{0,1:T(1,128)S(1)} %get-tuple-element.37, f32[8,1]{0,1:T(1,128)S(1)} %get-tuple-element.38, f32[]{:T(128)S(6)} %div.22, f32[8,32,2048]{2,1,0:T(8,128)} %param.7), kind=kOutput, calls=%fused_computation.7 | convolution fusion | flops 14680096 | bytes 6815816 | tf_op jit(solution)/shard_map/tm,mab->tab/dot_general | solution.py:57
  91.0 1.9 %collective-permute-start.2 = (f32[8,1,2048]{2,0,1:T(8,128)S(1)}, f32[8,1,2048]{2,0,1:T(8,128)S(1)}, u32[]{:S(2)}, u32[]{:S(2)}) collective-permute-start(f32[8,1,2048]{2,0,1:T(8,128)S(1)} %get-tuple-element.29), channel_id=1, source_target_pairs={{1,0},{2,1},{3,2},{4,3},{5,4},{6,5},{7,6},{9,8},{10,9},{11,10},{12... | collective-permute-start | bytes 196616 | tf_op jit(solution)/shard_map/ppermute | solution.py:16
  92.9 3.9 %collective-permute-start.3 = (f32[8,1,2048]{2,0,1:T(8,128)S(1)}, f32[8,1,2048]{2,0,1:T(8,128)S(1)}, u32[]{:S(2)}, u32[]{:S(2)}) collective-permute-start(f32[8,1,2048]{2,0,1:T(8,128)S(1)} %get-tuple-element.30), channel_id=1, source_target_pairs={{0,1},{1,2},{2,3},{3,4},{4,5},{5,6},{6,7},{8,9},{9,10},{10,11},{11... | collective-permute-start | bytes 196616 | tf_op jit(solution)/shard_map/ppermute | solution.py:15
  97.1 4.0 %collective-permute-done.3 = f32[8,1,2048]{2,0,1:T(8,128)S(1)} collective-permute-done((f32[8,1,2048]{2,0,1:T(8,128)S(1)}, f32[8,1,2048]{2,0,1:T(8,128)S(1)}, u32[]{:S(2)}, u32[]{:S(2)}) %collective-permute-start.3) | collective-permute-done | bytes 65568 | tf_op jit(solution)/shard_map/ppermute | solution.py:15
  101.2 2.4 %fusion.8 = f32[8,32,2048]{2,0,1:T(8,128)S(1)} fusion(f32[8,32,2048]{2,0,1:T(8,128)S(1)} %fusion.5, f32[8,1,2048]{2,0,1:T(8,128)S(1)} %collective-permute-done.3, f32[8,1,2048]{2,0,1:T(8,128)S(1)} %collective-permute-done.2, f32[]{:T(128)} %bitcast.5, pred[2048]{0:T(1024)(128)(4,1)S(1)} %get-tuple-element.33, pred[2048]{0:T(1024)(128)(4,1)S(1)} %get-tuple-element.34), kind=kLoop, calls=%fused_computation.13 | loop fusion | flops 7864320 | bytes 4329476 | tf_op jit(solution)/shard_map/sub | solution.py:51
  105.0 1.8 %fusion.43 = f32[2,32,2048]{2,0,1:T(2,128)S(1)} fusion(f32[8,32,2048]{2,0,1:T(8,128)S(1)} %fusion.8, f32[1,8]{1,0:T(1,128)S(1)} %get-tuple-element.35, f32[1,8]{1,0:T(1,128)S(1)} %get-tuple-element.36), kind=kOutput, calls=%fused_computation.70 | convolution fusion | flops 12582928 | bytes 2621504 | tf_op jit(solution)/shard_map/ms,sab->mab/dot_general | solution.py:52
  106.8 22.5 %all_to_all.66 = f32[2,32,2048]{2,0,1:T(2,128)S(1)} all-to-all(f32[2,32,2048]{2,0,1:T(2,128)S(1)} %fusion.43), channel_id=1, replica_groups=mesh['tm'=32,'space'=8] {'tm'}, dimensions={1} | all-to-all | bytes 1048576 | tf_op jit(solution)/shard_map/all_to_all | solution.py:53
  131.5 5.0 %all-to-all-start.3 = ((f32[64,1,2048]{2,1,0:T(1,128)}), f32[64,1,2048]{2,1,0:T(1,128)S(1)}, u32[]{:S(2)}, u32[]{:S(2)}) async-start(f32[64,1,2048]{2,1,0:T(1,128)} %copy.51), calls=%async_computation.3 | async-start | bytes 1048576 | tf_op jit(solution)/shard_map/all_to_all | solution.py:55
  136.5 4.7 %fusion.34 = f32[8,32,2048]{2,0,1:T(8,128)} fusion(f32[8,32,2048]{2,0,1:T(8,128)} %copy-done, f32[]{:T(128)S(6)} %neg.4, f32[]{:T(128)S(6)} %div.22), kind=kOutput, calls=%fused_computation.54 | convolution fusion | flops 50331968 | bytes 4194312 | tf_op jit(solution)/shard_map/ts,sab->tab/dot_general | solution.py:56
  141.2 12.9 %all-to-all-done.3 = f32[64,1,2048]{2,1,0:T(1,128)S(1)} async-done(((f32[64,1,2048]{2,1,0:T(1,128)}), f32[64,1,2048]{2,1,0:T(1,128)S(1)}, u32[]{:S(2)}, u32[]{:S(2)}) %all-to-all-start.3) | async-done | bytes 524320 | tf_op jit(solution)/shard_map/all_to_all | solution.py:55
  155.7 4.0 %fusion.2 = f32[8,32,2048]{2,0,1:T(8,128)S(1)} fusion(f32[8,32,2048]{2,0,1:T(8,128)S(1)} %fusion.5, f32[8,32,2048]{2,0,1:T(8,128)} %fusion.34, f32[]{:T(128)} %bitcast.53, f32[32,2,1,2048]{3,1,0,2:T(2,128)S(1)} %all_to_all.59, f32[8,1]{0,1:T(1,128)S(1)} %get-tuple-element.37, f32[8,1]{0,1:T(1,128)S(1)} %get-tuple-element.38, f32[]{:T(128)S(6)} %div.22), kind=kOutput, calls=%fused_computation.3 | convolution fusion | flops 14680096 | bytes 6815816 | tf_op jit(solution)/shard_map/tm,mab->tab/dot_general | solution.py:57
  159.8 2.5 %copy.52 = f32[8,32,2048]{2,1,0:T(8,128)} copy(f32[8,32,2048]{2,0,1:T(8,128)S(1)} %fusion.2) | data formatting | bytes 4194304 | tf_op jit(solution)/shard_map/sub | solution.py:58
  (25 shorter events, 11.4 us)
Async XLA Ops:
  2.8 1.3 copy-start.1
  4.1 8.0 %collective-permute-start = (f32[8,1,2048]{2,0,1:T(8,128)S(1)}, f32[8,1,2048]{2,0,1:T(8,128)S(1)}, u32[]{:S(2)}, u32[]{:S(2)}) collective-permute-start(f32[8,1,2048]{2,0,1:T(8,128)S(1)} %get-tuple-element.31), channel_id=1, source_target_pairs={{1,0},{2,1},{3,2},{4,3},{5,4},{6,5},{7,6},{9,8},{10,9},{11,10},{12... | collective-permute-start | bytes 196616 | tf_op jit(solution)/shard_map/ppermute | solution.py:16
  9.3 8.3 %collective-permute-start.1 = (f32[8,1,2048]{2,0,1:T(8,128)S(1)}, f32[8,1,2048]{2,0,1:T(8,128)S(1)}, u32[]{:S(2)}, u32[]{:S(2)}) collective-permute-start(f32[8,1,2048]{2,0,1:T(8,128)S(1)} %get-tuple-element.32), channel_id=1, source_target_pairs={{0,1},{1,2},{2,3},{3,4},{4,5},{5,6},{6,7},{8,9},{9,10},{10,11},{11... | collective-permute-start | bytes 196616 | tf_op jit(solution)/shard_map/ppermute | solution.py:15
  28.8 29.4 %all-to-all-start = ((f32[2,32,2048]{2,0,1:T(2,128)}), f32[2,32,2048]{2,0,1:T(2,128)}, u32[]{:S(2)}, u32[]{:S(2)}) async-start(f32[2,32,2048]{2,0,1:T(2,128)} %fusion.44), calls=%async_computation | async-start | bytes 1048576 | tf_op jit(solution)/shard_map/all_to_all | solution.py:53
  61.4 22.7 %all-to-all-start.1 = ((f32[64,1,2048]{2,1,0:T(1,128)}), f32[64,1,2048]{2,1,0:T(1,128)S(1)}, u32[]{:S(2)}, u32[]{:S(2)}) async-start(f32[64,1,2048]{2,1,0:T(1,128)} %copy.48), calls=%async_computation.1 | async-start | bytes 1048576 | tf_op jit(solution)/shard_map/all_to_all | solution.py:55
  91.0 6.2 %collective-permute-start.2 = (f32[8,1,2048]{2,0,1:T(8,128)S(1)}, f32[8,1,2048]{2,0,1:T(8,128)S(1)}, u32[]{:S(2)}, u32[]{:S(2)}) collective-permute-start(f32[8,1,2048]{2,0,1:T(8,128)S(1)} %get-tuple-element.29), channel_id=1, source_target_pairs={{1,0},{2,1},{3,2},{4,3},{5,4},{6,5},{7,6},{9,8},{10,9},{11,10},{12... | collective-permute-start | bytes 196616 | tf_op jit(solution)/shard_map/ppermute | solution.py:16
  92.9 8.3 %collective-permute-start.3 = (f32[8,1,2048]{2,0,1:T(8,128)S(1)}, f32[8,1,2048]{2,0,1:T(8,128)S(1)}, u32[]{:S(2)}, u32[]{:S(2)}) collective-permute-start(f32[8,1,2048]{2,0,1:T(8,128)S(1)} %get-tuple-element.30), channel_id=1, source_target_pairs={{0,1},{1,2},{2,3},{3,4},{4,5},{5,6},{6,7},{8,9},{9,10},{10,11},{11... | collective-permute-start | bytes 196616 | tf_op jit(solution)/shard_map/ppermute | solution.py:15
  103.6 1.3 copy-start
  131.5 22.7 %all-to-all-start.3 = ((f32[64,1,2048]{2,1,0:T(1,128)}), f32[64,1,2048]{2,1,0:T(1,128)S(1)}, u32[]{:S(2)}, u32[]{:S(2)}) async-start(f32[64,1,2048]{2,1,0:T(1,128)} %copy.51), calls=%async_computation.3 | async-start | bytes 1048576 | tf_op jit(solution)/shard_map/all_to_all | solution.py:55

commit v2 on v1

v2 whole, which is shorter than its diff:
```python
import functools

import jax
import jax.numpy as jnp
from jax import lax
from jax.experimental import pallas as pl
from jax.experimental.pallas import tpu as pltpu
from jax.sharding import PartitionSpec as P

NZ = 32
ITERS = 2
LANES = 128
ROWS = 8
MESH = pl.DeviceIdType.MESH


def kernel(nz, ny, nc, slices, step_ref, mass_ref, field, out, fb, gb, hb, mom, u1, xs, xr, zs, zr, ws, wr, vs, vr, cs, yv,
           load_sem, store_sem, send, recv, hsend, hrecv):
    tiles = fb.shape[1] - 2
    groups = fb.shape[2] // ROWS
    kt = tiles // nc
    tm, sp = lax.axis_index("tm"), lax.axis_index("space")
    z, h, c = tm // 4, (tm // 2) % 2, tm % 2
    lo, y = sp // ny, sp % ny
    last = 2 * ny - 1
    other = (tm + 1 - 2 * c, sp)
    side = lambda hd: (z * 4 + hd * 2 + c, (1 - lo) * ny + y)
    along = lambda d: ((tm + 4 * d) % (4 * nz), sp)
    has_left, has_right = sp > 0, sp < last

    barrier = pltpu.get_barrier_semaphore()

    def greet(device):
        pl.semaphore_signal(barrier, inc=1, device_id=device, device_id_type=MESH)

    greet(other)
    greet(side(0))
    greet(side(1))
    for d in range(1, nz):
        greet(along(d))

    @pl.when(has_left)
    def _():
        greet((tm, sp - 1))

    @pl.when(has_right)
    def _():
        greet((tm, sp + 1))

    loads = [
        pltpu.make_async_copy(
            field.at[:, :, pl.ds(k * LANES, LANES)], fb.at[:, k + 1], load_sem.at[k]
        )
        for k in range(tiles)
    ]
    for load in loads:
        load.start()

    full = lambda value: jnp.full((ROWS, LANES), value, jnp.float32)
    blank = full(0.0)

    @pl.loop(0, slices)
    def _(t):
        for i in range(groups):
            fb[t, 0, pl.ds(i * ROWS, ROWS), :] = blank
            fb[t, tiles + 1, pl.ds(i * ROWS, ROWS), :] = blank

    def clear(which):
        @pl.loop(0, slices)
        def _(t):
            for it in range(ITERS):
                for ch in range(nc):
                    for k in range(kt):
                        hb[it, which, ch, t, k] = blank

    pl.when(jnp.logical_not(has_left))(lambda: clear(0))
    pl.when(jnp.logical_not(has_right))(lambda: clear(1))

    m = full(mass_ref[0])
    s = full(step_ref[0])
    m2 = m * m
    q = m * jnp.sqrt(1.0 + 0.25 * m2) - 0.5 * m2
    double = lambda p: p * (2.0 - p)
    r = 1.0 - q
    q8 = double(double(double(q)))
    q16 = double(q8)
    q32 = double(q16)
    r8, r16, r32 = 1.0 - q8, 1.0 - q16, 1.0 - q32
    whole = q32
    for _ in range((nz - 1).bit_length()):
        whole = double(whole)
    inv = 1.0 / whole
    linear = 7.0 - m2
    keep = 1.0 - s
    gain = s * r / (q * (1.0 + r))
    first = c == 0
    one = full(1.0)
    wa, wb = jnp.where(first, r8, one), jnp.where(first, one, r8)
    za, zb = jnp.where(first, one, blank), jnp.where(first, blank, one)

    lane = lax.broadcasted_iota(jnp.int32, (ROWS, LANES), 1)
    row = lax.broadcasted_iota(jnp.int32, (ROWS, LANES), 0)
    zplace = lane % NZ
    at_first, at_last = zplace == 0, zplace == NZ - 1
    low, high = lane < NZ, lane >= LANES - NZ
    top, bottom = row == 0, row == ROWS - 1

    def stencil(it, ch, which):
        @pl.loop(0, kt)
        def _(k):
            kk = ch * kt + k
            for i in which:
                rows = pl.ds(i * ROWS, ROWS)
                gs = []
                for t in range(slices):
                    f = fb[t, kk + 1, rows, :]
                    if i == 0:
                        xm = jnp.where(top, hb[it, 0, ch, t, k], pltpu.roll(f, 1, 0))
                    else:
                        xm = fb[t, kk + 1, pl.ds(i * ROWS - 1, ROWS), :]
                    if i == groups - 1:
                        xp = jnp.where(bottom, hb[it, 1, ch, t, k], pltpu.roll(f, ROWS - 1, 0))
                    else:
                        xp = fb[t, kk + 1, pl.ds(i * ROWS + 1, ROWS), :]
                    yp = pltpu.roll(jnp.where(low, fb[t, kk + 2, rows, :], f), LANES - NZ, 1)
                    ym = pltpu.roll(jnp.where(high, fb[t, kk, rows, :], f), NZ, 1)
                    zp = pltpu.roll(jnp.where(at_first, 0.0, f), LANES - 1, 1)
                    zm = pltpu.roll(jnp.where(at_last, 0.0, f), 1, 1)
                    near = (xm + xp) + (yp + ym) + (zp + zm)
                    g = f * (linear + f * (0.25 * f - 0.9)) - near
                    gb[t, kk, rows, :] = g
                    gs.append(g)
                before, after = gs[0], gs[-1]
                for t in range(1, slices):
                    before = r * before + gs[t]
                    after = r * after + gs[slices - 1 - t]
                mom[it, ch, i // 2, i % 2, 0, k] = before
                mom[it, ch, i // 2, i % 2, 1, k] = after

    def solve(it, ch):
        @pl.loop(0, kt)
        def _(k):
            kk = ch * kt + k
            for i in range(groups):
                rows = pl.ds(i * ROWS, ROWS)
                gs = [gb[t, kk, rows, :] for t in range(slices)]
                state = yv[it, ch, i // 2, i % 2, 0, k]
                states = []
                for t in range(slices):
                    state = r * state + gs[t]
                    states.append(state)
                ahead = r * yv[it, ch, i // 2, i % 2, 1, k]
                for t in reversed(range(slices)):
                    f = fb[t, kk + 1, rows, :]
                    fb[t, kk + 1, rows, :] = keep * f - gain * (states[t] + ahead)
                    ahead = r * (gs[t] + ahead)

    pending = []

    def copy(src, dst, send_sem, recv_sem, device):
        return pltpu.make_async_remote_copy(
            src_ref=src, dst_ref=dst, send_sem=send_sem, recv_sem=recv_sem, device_id=device, device_id_type=MESH
        )

    def start(src, dst, it, ch, a, b, device):
        one_copy = copy(src, dst, send.at[it, ch, a], recv.at[it, ch, b], device)
        one_copy.start()
        pending.append(one_copy)

    def arrive(dst, it, ch, b):
        copy(dst, dst, send.at[it, ch, b], recv.at[it, ch, b], other).wait_recv()

    def halo(it, ch, which):
        row_from, row_to = (groups * ROWS - 1, 0) if which == 0 else (0, ROWS - 1)
        return copy(
            fb.at[:, pl.ds(1 + ch * kt, kt), pl.ds(row_from, 1), :],
            hb.at[it, which, ch, :, :, pl.ds(row_to, 1), :],
            hsend.at[it, which, ch],
            hrecv.at[it, which, ch],
            (tm, sp + 1) if which == 0 else (tm, sp - 1),
        )

    def send_halo(it, ch):
        pl.when(has_right)(lambda: halo(it, ch, 0).start())
        pl.when(has_left)(lambda: halo(it, ch, 1).start())

    def sent_halo(it, ch):
        pl.when(has_right)(lambda: halo(it, ch, 0).wait_send())
        pl.when(has_left)(lambda: halo(it, ch, 1).wait_send())

    def wait_halo(it, ch):
        pl.when(has_left)(lambda: halo(it, ch, 0).wait_recv())
        pl.when(has_right)(lambda: halo(it, ch, 1).wait_recv())

    def up_core(it, ch):
        start(mom.at[it, ch, 1 - c], u1.at[it, ch], it, ch, 0, 0, other)

    def up_side(it, ch):
        arrive(u1.at[it, ch], it, ch, 0)

        @pl.loop(0, kt)
        def _(k):
            for hd in range(2):
                xs[it, ch, hd, 0, k] = wa * mom[it, ch, c, hd, 0, k] + wb * u1[it, ch, hd, 0, k]
                xs[it, ch, hd, 1, k] = wb * mom[it, ch, c, hd, 1, k] + wa * u1[it, ch, hd, 1, k]

        for hd in range(2):
            start(xs.at[it, ch, hd], xr.at[it, ch, h], it, ch, 1 + hd, 1 + h, side(hd))

    far_first = sorted(range(1, nz), key=lambda d: (-min(d, nz - d), d))

    def up_along(it, ch):
        for hs in range(2):
            arrive(xr.at[it, ch, hs], it, ch, 1 + hs)

        @pl.loop(0, kt)
        def _(k):
            zs[it, ch, k, 0] = r16 * xr[it, ch, 0, 0, k] + xr[it, ch, 1, 0, k]
            zs[it, ch, k, 1] = xr[it, ch, 0, 1, k] + r16 * xr[it, ch, 1, 1, k]

        for d in far_first:
            start(zs.at[it, ch, (z + d) % nz], zr.at[it, ch, z], it, ch, 2 + d, 2 + d, along(d))
        zr[it, ch, z] = zs[it, ch, z]

    def down_along(it, ch):
        for d in far_first:
            arrive(zr.at[it, ch, (z + nz - d) % nz], it, ch, 2 + d)
        ms = [zr[it, ch, j, 0] for j in range(nz)]
        ns = [zr[it, ch, j, 1] for j in range(nz)]
        before, after = ms[0], ns[-1]
        for j in range(1, nz):
            before = r32 * before + ms[j]
            after = r32 * after + ns[nz - 1 - j]
        before, after = inv * before, inv * after
        for j in range(nz):
            ws[it, ch, j, 0] = before
            ws[it, ch, nz - 1 - j, 1] = after
            before = r32 * before + ms[j]
            after = r32 * after + ns[nz - 1 - j]
        for d in far_first:
            start(ws.at[it, ch, (z + d) % nz], wr.at[it, ch, z], it, ch, 1 + nz + d, 1 + nz + d, along(d))
        wr[it, ch, z] = ws[it, ch, z]

    def down_side(it, ch):
        for d in far_first:
            arrive(wr.at[it, ch, (z + nz - d) % nz], it, ch, 1 + nz + d)

        @pl.loop(0, kt)
        def _(k):
            before, after = wr[it, ch, k, 0], wr[it, ch, k, 1]
            vs[it, ch, 0, 0, k] = before
            vs[it, ch, 0, 1, k] = xr[it, ch, 1, 1, k] + r16 * after
            vs[it, ch, 1, 0, k] = xr[it, ch, 0, 0, k] + r16 * before
            vs[it, ch, 1, 1, k] = after

        for hd in range(2):
            start(vs.at[it, ch, hd], vr.at[it, ch, h], it, ch, 1 + 2 * nz + hd, 1 + 2 * nz + h, side(hd))

    def down_core(it, ch):
        for hs in range(2):
            arrive(vr.at[it, ch, hs], it, ch, 1 + 2 * nz + hs)

        @pl.loop(0, kt)
        def _(k):
            for hd in range(2):
                before, after = vr[it, ch, hd, 0, k], vr[it, ch, hd, 1, k]
                cs[it, ch, hd, 0, k] = wa * before + za * mom[it, ch, c, hd, 0, k]
                cs[it, ch, hd, 1, k] = wb * after + zb * mom[it, ch, c, hd, 1, k]
                yv[it, ch, c, hd, 0, k] = wb * before + zb * u1[it, ch, hd, 0, k]
                yv[it, ch, c, hd, 1, k] = wa * after + za * u1[it, ch, hd, 1, k]

        start(cs.at[it, ch], yv.at[it, ch, c], it, ch, 3 + 2 * nz, 3 + 2 * nz, other)

    inner, outer = tuple(range(1, groups - 1)), (0, groups - 1)
    for load in loads:
        load.wait()
    stores = []
    for it in range(ITERS):
        if it == 0:
            stencil(it, 0, inner)
            pl.semaphore_wait(barrier, nz + 2 + has_left.astype(jnp.int32) + has_right.astype(jnp.int32))
            for ch in range(nc):
                send_halo(it, ch)
        else:
            stencil(it, 0, inner)
        for ch in range(1, nc):
            stencil(it, ch, inner)
        for ch in range(nc):
            wait_halo(it, ch)
            stencil(it, ch, outer)
            up_core(it, ch)
        for phase in (up_side, up_along, down_along, down_side, down_core):
            for ch in range(nc):
                phase(it, ch)
        for ch in range(nc):
            arrive(yv.at[it, ch, 1 - c], it, ch, 3 + 2 * nz)
            sent_halo(it, ch)
            solve(it, ch)
            if it + 1 < ITERS:
                send_halo(it + 1, ch)
            else:
                for k in range(ch * kt, (ch + 1) * kt):
                    store = pltpu.make_async_copy(
                        fb.at[:, k + 1], out.at[:, :, pl.ds(k * LANES, LANES)], store_sem.at[k]
                    )
                    store.start()
                    stores.append(store)
    for one_copy in pending:
        one_copy.wait_send()
    for store in stores:
        store.wait()


def solution(mesh):
    nz = mesh.shape["tm"] // 4
    ny = mesh.shape["space"] // 2

    def on_device(field, step, mass):
        slices, planes, width = field.shape
        tiles = width // LANES
        nc = tiles // nz
        groups = planes // ROWS
        tile = (ROWS, LANES)
        vmem = lambda *shape: pltpu.VMEM(shape, jnp.float32)
        level = (ITERS, nc)
        sems = 4 + 2 * nz
        return pl.pallas_call(
            functools.partial(kernel, nz, ny, nc, slices),
            out_shape=jax.ShapeDtypeStruct(field.shape, field.dtype),
            in_specs=[
                pl.BlockSpec(memory_space=pltpu.SMEM),
                pl.BlockSpec(memory_space=pltpu.SMEM),
                pl.BlockSpec(memory_space=pl.ANY),
            ],
            out_specs=pl.BlockSpec(memory_space=pl.ANY),
            scratch_shapes=[
                vmem(slices, tiles + 2, planes, LANES),
                vmem(slices, tiles, planes, LANES),
                vmem(ITERS, 2, nc, slices, nz, *tile),
                vmem(*level, 2, 2, 2, nz, *tile),
                vmem(*level, 2, 2, nz, *tile),
                vmem(*level, 2, 2, nz, *tile),
                vmem(*level, 2, 2, nz, *tile),
                vmem(*level, nz, 2, *tile),
                vmem(*level, nz, 2, *tile),
                vmem(*level, nz, 2, *tile),
                vmem(*level, nz, 2, *tile),
                vmem(*level, 2, 2, nz, *tile),
                vmem(*level, 2, 2, nz, *tile),
                vmem(*level, 2, 2, nz, *tile),
                vmem(*level, 2, 2, 2, nz, *tile),
                pltpu.SemaphoreType.DMA((tiles,)),
                pltpu.SemaphoreType.DMA((tiles,)),
                pltpu.SemaphoreType.DMA((*level, sems)),
                pltpu.SemaphoreType.DMA((*level, sems)),
                pltpu.SemaphoreType.DMA((ITERS, 2, nc)),
                pltpu.SemaphoreType.DMA((ITERS, 2, nc)),
            ],
            compiler_params=pltpu.CompilerParams(
                collective_id=0, has_side_effects=True, vmem_limit_bytes=48 * 1024 * 1024
            ),
        )(step, mass, field)

    return jax.shard_map(
        on_device,
        mesh=mesh,
        in_specs=(P("tm", "space", None), P(), P()),
        out_specs=P("tm", "space", None),
        check_vma=False,
    )
```

time: 163 us -> 67.9 us (0.42)
  the two profiles are of different devices: /device:TPU:6 before, /device:TPU:1 now
where the time goes in v2:
time: 67.9 us; the launch traced here: 66.9 us
  Pallas kernels  62.7 us (92%)
  local copies, waits for them, and re-layouts  2.91 us (4%)
  between operations  1.31 us (2%)
    pallas_call x1, Pallas kernels, on_device(): pl.pallas_call(functools.partial(kernel, nz, ny, nc, slices), out_shape=j...  62.7 us
    unnamed x3, local copies, waits for them, and re-layouts  2.91 us

profile of v2, /device:TPU:1, one launch (start us, length us, event | category | flops | bytes accessed | tf_op | source)
XLA Modules:
  0.0 66.9 jit_solution(3263035590452071394)
XLA Ops:
  1.3 0.0 copy-start
  1.3 1.6 %copy-done = f32[8,32,2048]{2,1,0:T(8,128)S(1)} copy-done((f32[8,32,2048]{2,1,0:T(8,128)S(1)}, f32[8,32,2048]{2,1,0:T(8,128)}, u32[]{:S(2)}) %copy-start) | copy-done | bytes 2097176
  2.9 62.7 %shard_map.37 = f32[8,32,2048]{2,1,0:T(8,128)S(1)} custom-call(f32[1]{0:T(128)S(6)} %copy.5.step_ref, f32[1]{0:T(128)S(6)} %copy.6.mass_ref, f32[8,32,2048]{2,1,0:T(8,128)S(1)} %copy-done), custom_call_target="tpu_custom_call" | custom-call | tf_op jit(solution)/shard_map/pallas_call | solution.py:327
  65.6 1.3 %copy.7 = f32[8,32,2048]{2,1,0:T(8,128)} copy(f32[8,32,2048]{2,1,0:T(8,128)S(1)} %shard_map.37) | data formatting | bytes 4194304
Async XLA Ops:
  1.3 1.6 %copy-start = (f32[8,32,2048]{2,1,0:T(8,128)S(1)}, f32[8,32,2048]{2,1,0:T(8,128)}, u32[]{:S(2)}) copy-start(f32[8,32,2048]{2,1,0:T(8,128)} %field.1) | copy-start | bytes 6291460

commit v3 on v1

v3 whole, which is shorter than its diff:
```python
import functools

import jax
import jax.numpy as jnp
from jax import lax
from jax.experimental import pallas as pl
from jax.experimental.pallas import tpu as pltpu
from jax.sharding import PartitionSpec as P

NZ = 32
ITERS = 2
VMEM_MIB = 40
LANES = 128
ROWS = 8
MESH = pl.DeviceIdType.MESH


def kernel(nz, ny, slices, step_ref, mass_ref, field, out, fb, gb, hs, hb, mom, u1, xs, zr, ws, wr, cs, yv,
           load_sem, send, recv, hsend, hrecv):
    tiles = fb.shape[1] - 2
    groups = fb.shape[2] // ROWS
    tm, sp = lax.axis_index("tm"), lax.axis_index("space")
    z, h, c = tm // 4, (tm // 2) % 2, tm % 2
    lo, y = sp // ny, sp % ny
    last = 2 * ny - 1
    other = (tm + 1 - 2 * c, sp)
    owner = lambda d, hd: (((z + d) % nz) * 4 + hd * 2 + c, (1 - lo) * ny + y)
    has_left, has_right = sp > 0, sp < last

    barrier = pltpu.get_barrier_semaphore()

    def greet(device):
        pl.semaphore_signal(barrier, inc=1, device_id=device, device_id_type=MESH)

    far_first = sorted(range(nz), key=lambda d: (-min(d, nz - d), d))
    for d in far_first:
        for hd in range(2):
            greet(owner(d, hd))
    greet(other)

    @pl.when(has_left)
    def _():
        greet((tm, sp - 1))

    @pl.when(has_right)
    def _():
        greet((tm, sp + 1))

    loads = [
        pltpu.make_async_copy(
            field.at[:, :, pl.ds(k * LANES, LANES)], fb.at[:, k + 1], load_sem.at[k]
        )
        for k in range(tiles)
    ]
    for load in loads:
        load.start()

    full = lambda value: jnp.full((ROWS, LANES), value, jnp.float32)
    blank = full(0.0)

    for t in range(slices):
        for i in range(groups):
            fb[t, 0, pl.ds(i * ROWS, ROWS), :] = blank
            fb[t, tiles + 1, pl.ds(i * ROWS, ROWS), :] = blank

    def clear(which):
        for it in range(ITERS):
            hb[it, which] = jnp.zeros(hb.shape[2:], jnp.float32)

    pl.when(jnp.logical_not(has_left))(lambda: clear(0))
    pl.when(jnp.logical_not(has_right))(lambda: clear(1))

    m = full(mass_ref[0])
    s = full(step_ref[0])
    m2 = m * m
    q = m * jnp.sqrt(1.0 + 0.25 * m2) - 0.5 * m2
    double = lambda p: p * (2.0 - p)
    r = 1.0 - q
    q8 = double(double(double(q)))
    q16 = double(q8)
    r8, r16 = 1.0 - q8, 1.0 - q16
    whole = q16
    for _ in range((2 * nz - 1).bit_length()):
        whole = double(whole)
    inv = 1.0 / whole
    linear = 7.0 - m2
    keep = 1.0 - s
    gain = s * r / (q * (1.0 + r))
    first = c == 0
    one = full(1.0)
    wa, wb = jnp.where(first, r8, one), jnp.where(first, one, r8)
    za, zb = jnp.where(first, one, blank), jnp.where(first, blank, one)

    lane = lax.broadcasted_iota(jnp.int32, (ROWS, LANES), 1)
    row = lax.broadcasted_iota(jnp.int32, (ROWS, LANES), 0)
    zplace = lane % NZ
    at_first, at_last = zplace == 0, zplace == NZ - 1
    low, high = lane < NZ, lane >= LANES - NZ
    top, bottom = row == 0, row == ROWS - 1

    parts = (tuple(range(1, groups - 1)), (0, groups - 1))

    def stencil(it, part):
        @pl.loop(0, tiles // 4)
        def _(quad):
            for k in (quad * 4 + j for j in range(4)):
                for half, i in enumerate(parts[part]):
                    rows = pl.ds(i * ROWS, ROWS)
                    gs = []
                    for t in range(slices):
                        f = fb[t, k + 1, rows, :]
                        if i == 0:
                            xm = jnp.where(top, hb[it, 0, t, pl.ds(k, 1), :], pltpu.roll(f, 1, 0))
                        else:
                            xm = fb[t, k + 1, pl.ds(i * ROWS - 1, ROWS), :]
                        if i == groups - 1:
                            xp = jnp.where(bottom, hb[it, 1, t, pl.ds(k, 1), :], pltpu.roll(f, ROWS - 1, 0))
                        else:
                            xp = fb[t, k + 1, pl.ds(i * ROWS + 1, ROWS), :]
                        yp = pltpu.roll(jnp.where(low, fb[t, k + 2, rows, :], f), LANES - NZ, 1)
                        ym = pltpu.roll(jnp.where(high, fb[t, k, rows, :], f), NZ, 1)
                        zp = pltpu.roll(jnp.where(at_first, 0.0, f), LANES - 1, 1)
                        zm = pltpu.roll(jnp.where(at_last, 0.0, f), 1, 1)
                        near = (xm + xp) + (yp + ym) + (zp + zm)
                        g = f * (linear + f * (0.25 * f - 0.9)) - near
                        gb[t, k, rows, :] = g
                        gs.append(g)
                    before, after = gs[0], gs[-1]
                    for t in range(1, slices):
                        before = r * before + gs[t]
                        after = r * after + gs[slices - 1 - t]
                    mom[it, part, half, k, 0] = before
                    mom[it, part, half, k, 1] = after

    def solve(it, part):
        @pl.loop(0, tiles // 4)
        def _(quad):
            for j in range(4):
                k = quad * 4 + j
                for half, i in enumerate(parts[part]):
                    rows = pl.ds(i * ROWS, ROWS)
                    gs = [gb[t, k, rows, :] for t in range(slices)]
                    state = yv[it, part, half, k, 0]
                    states = []
                    for t in range(slices):
                        state = r * state + gs[t]
                        states.append(state)
                    ahead = r * yv[it, part, half, k, 1]
                    for t in reversed(range(slices)):
                        new = keep * fb[t, k + 1, rows, :] - gain * (states[t] + ahead)
                        if it + 1 < ITERS:
                            fb[t, k + 1, rows, :] = new
                        else:
                            out[t, rows, pl.ds(pl.multiple_of(k * LANES, LANES), LANES)] = new
                        if it + 1 < ITERS and i == 0:
                            hs[it + 1, 1, t, pl.ds(k, 1), :] = new[:1]
                        if it + 1 < ITERS and i == groups - 1:
                            hs[it + 1, 0, t, pl.ds(k, 1), :] = new[ROWS - 1 :]
                        ahead = r * (gs[t] + ahead)

    pending = []

    def copy(src, dst, send_sem, recv_sem, device):
        return pltpu.make_async_remote_copy(
            src_ref=src, dst_ref=dst, send_sem=send_sem, recv_sem=recv_sem, device_id=device, device_id_type=MESH
        )

    def start(src, dst, it, part, a, b, device):
        one_copy = copy(src, dst, send.at[it, part, a], recv.at[it, part, b], device)
        one_copy.start()
        pending.append(one_copy)

    def arrive(dst, it, part, b):
        copy(dst, dst, send.at[it, part, b], recv.at[it, part, b], other).wait_recv()

    def pack(it):
        @pl.loop(0, slices)
        def _(t):
            for which, edge in enumerate((groups * ROWS - 1, 0)):
                for k in range(tiles):
                    hs[it, which, t, pl.ds(k, 1), :] = fb[t, k + 1, pl.ds(edge, 1), :]

    def halo(it, which):
        return copy(
            hs.at[it, which],
            hb.at[it, which],
            hsend.at[it, which],
            hrecv.at[it, which],
            (tm, sp + 1) if which == 0 else (tm, sp - 1),
        )

    def send_halo(it):
        pl.when(has_right)(lambda: halo(it, 0).start())
        pl.when(has_left)(lambda: halo(it, 1).start())

    def wait_halo(it):
        pl.when(has_left)(lambda: halo(it, 0).wait_recv())
        pl.when(has_right)(lambda: halo(it, 1).wait_recv())

    up = lambda d, hd: 1 + 2 * d + hd
    down = lambda d, hd: 1 + 2 * nz + 2 * d + hd
    back = 1 + 4 * nz

    def up_core(it, part):
        start(mom.at[it, part, 1 - c], u1.at[it, part], it, part, 0, 0, other)

    def up_owner(it, part):
        arrive(u1.at[it, part], it, part, 0)
        for k in range(tiles):
            xs[it, part, k, 0] = wa * mom[it, part, c, k, 0] + wb * u1[it, part, k, 0]
            xs[it, part, k, 1] = wb * mom[it, part, c, k, 1] + wa * u1[it, part, k, 1]
        for d in far_first:
            for hd in range(2):
                src = xs.at[it, part, hd * nz + (z + d) % nz]
                start(src, zr.at[it, part, z * 2 + h], it, part, up(d, hd), up(d, h), owner(d, hd))

    def down_owner(it, part):
        for d in reversed(far_first):
            for hd in range(2):
                arrive(zr.at[it, part, ((z + nz - d) % nz) * 2 + hd], it, part, up(d, hd))
        ms = [zr[it, part, j, 0] for j in range(2 * nz)]
        ns = [zr[it, part, j, 1] for j in range(2 * nz)]
        left, right, ratio = ms, ns, r16
        while len(left) > 1:
            pairs = range(0, len(left), 2)
            left = [ratio * left[j] + left[j + 1] for j in pairs]
            right = [right[j] + ratio * right[j + 1] for j in pairs]
            ratio = ratio * ratio
        before, after = inv * left[0], inv * right[0]
        for j in range(2 * nz):
            ws[it, part, j, 0] = before
            ws[it, part, 2 * nz - 1 - j, 1] = after
            before = r16 * before + ms[j]
            after = r16 * after + ns[2 * nz - 1 - j]
        for d in far_first:
            for hd in range(2):
                src = ws.at[it, part, ((z + d) % nz) * 2 + hd]
                start(src, wr.at[it, part, h * nz + z], it, part, down(d, hd), down(d, h), owner(d, hd))

    def down_core(it, part):
        for d in reversed(far_first):
            for hd in range(2):
                arrive(wr.at[it, part, hd * nz + (z + nz - d) % nz], it, part, down(d, hd))
        for k in range(tiles):
            before, after = wr[it, part, k, 0], wr[it, part, k, 1]
            cs[it, part, k, 0] = wa * before + za * mom[it, part, c, k, 0]
            cs[it, part, k, 1] = wb * after + zb * mom[it, part, c, k, 1]
        start(cs.at[it, part], yv.at[it, part, c], it, part, back, back, other)
        for k in range(tiles):
            before, after = wr[it, part, k, 0], wr[it, part, k, 1]
            yv[it, part, c, k, 0] = wb * before + zb * u1[it, part, k, 0]
            yv[it, part, c, k, 1] = wa * after + za * u1[it, part, k, 1]

    for load in loads:
        load.wait()
    pack(0)
    stencil(0, 0)
    pl.semaphore_wait(barrier, 2 * nz + 1 + has_left.astype(jnp.int32) + has_right.astype(jnp.int32))
    send_halo(0)
    for it in range(ITERS):
        up_core(it, 0)
        wait_halo(it)
        stencil(it, 1)
        up_core(it, 1)
        for phase in (up_owner, down_owner, down_core):
            for part in range(2):
                phase(it, part)
        for part in range(2):
            arrive(yv.at[it, part, 1 - c], it, part, back)
            solve(it, part)
        if it + 1 < ITERS:
            send_halo(it + 1)
            stencil(it + 1, 0)
    for one_copy in pending:
        one_copy.wait_send()
    for it in range(ITERS):
        pl.when(has_right)(lambda: halo(it, 0).wait_send())
        pl.when(has_left)(lambda: halo(it, 1).wait_send())


def solution(mesh):
    nz = mesh.shape["tm"] // 4
    ny = mesh.shape["space"] // 2

    def on_device(field, step, mass):
        slices, planes, width = field.shape
        tiles = width // LANES
        tile = (ROWS, LANES)
        vmem = lambda *shape: pltpu.VMEM(shape, jnp.float32)
        level = (ITERS, 2)
        sems = 2 + 4 * nz
        return pl.pallas_call(
            functools.partial(kernel, nz, ny, slices),
            out_shape=jax.ShapeDtypeStruct(field.shape, field.dtype),
            in_specs=[
                pl.BlockSpec(memory_space=pltpu.SMEM),
                pl.BlockSpec(memory_space=pltpu.SMEM),
                pl.BlockSpec(memory_space=pltpu.HBM),
            ],
            out_specs=pl.BlockSpec(memory_space=pltpu.VMEM),
            scratch_shapes=[
                vmem(slices, tiles + 2, planes, LANES),
                vmem(slices, tiles, planes, LANES),
                vmem(ITERS, 2, slices, tiles, LANES),
                vmem(ITERS, 2, slices, tiles, LANES),
                vmem(*level, 2, tiles, 2, *tile),
                vmem(*level, tiles, 2, *tile),
                vmem(*level, tiles, 2, *tile),
                vmem(*level, tiles, 2, *tile),
                vmem(*level, tiles, 2, *tile),
                vmem(*level, tiles, 2, *tile),
                vmem(*level, tiles, 2, *tile),
                vmem(*level, 2, tiles, 2, *tile),
                pltpu.SemaphoreType.DMA((tiles,)),
                pltpu.SemaphoreType.DMA((*level, sems)),
                pltpu.SemaphoreType.DMA((*level, sems)),
                pltpu.SemaphoreType.DMA((ITERS, 2)),
                pltpu.SemaphoreType.DMA((ITERS, 2)),
            ],
            compiler_params=pltpu.CompilerParams(
                collective_id=0, has_side_effects=True, vmem_limit_bytes=VMEM_MIB * 1024 * 1024
            ),
        )(step, mass, field)

    return jax.shard_map(
        on_device,
        mesh=mesh,
        in_specs=(P("tm", "space", None), P(), P()),
        out_specs=P("tm", "space", None),
        check_vma=False,
    )
```

time: 163 us -> 61.8 us (0.38)
  the two profiles are of different devices: /device:TPU:6 before, /device:TPU:1 now
where the time goes in v3:
time: 61.8 us; the launch traced here: 61.7 us
  Pallas kernels  57.5 us (93%)
  local copies, waits for them, and re-layouts  2.91 us (5%)
  between operations  1.31 us (2%)
    pallas_call x1, Pallas kernels, on_device(): pl.pallas_call(functools.partial(kernel, nz, ny, slices), out_shape=jax.S...  57.5 us
    unnamed x3, local copies, waits for them, and re-layouts  2.91 us

profile of v3, /device:TPU:1, one launch (start us, length us, event | category | flops | bytes accessed | tf_op | source)
XLA Modules:
  0.0 61.7 jit_solution(17584729798565692269)
XLA Ops:
  1.3 0.0 copy-start
  1.3 1.6 %copy-done = f32[8,32,2048]{2,1,0:T(8,128)S(1)} copy-done((f32[8,32,2048]{2,1,0:T(8,128)S(1)}, f32[8,32,2048]{2,1,0:T(8,128)}, u32[]{:S(2)}) %copy-start) | copy-done | bytes 2097176
  2.9 57.5 %shard_map.37 = f32[8,32,2048]{2,1,0:T(8,128)S(1)} custom-call(f32[1]{0:T(128)S(6)} %copy.5.step_ref, f32[1]{0:T(128)S(6)} %copy.6.mass_ref, f32[8,32,2048]{2,1,0:T(8,128)S(1)} %copy-done), custom_call_target="tpu_custom_call" | custom-call | tf_op jit(solution)/shard_map/pallas_call | solution.py:292
  60.4 1.3 %copy.7 = f32[8,32,2048]{2,1,0:T(8,128)} copy(f32[8,32,2048]{2,1,0:T(8,128)S(1)} %shard_map.37) | data formatting | bytes 4194304
Async XLA Ops:
  1.3 1.6 %copy-start = (f32[8,32,2048]{2,1,0:T(8,128)S(1)}, f32[8,32,2048]{2,1,0:T(8,128)}, u32[]{:S(2)}) copy-start(f32[8,32,2048]{2,1,0:T(8,128)} %field.1) | copy-start | bytes 6291460

commit v4 on v3

--- a/solution.py
+++ b/solution.py
@@ -259,10 +259,12 @@
     send_halo(0)
     for it in range(ITERS):
         up_core(it, 0)
+        up_owner(it, 0)
         wait_halo(it)
         stencil(it, 1)
         up_core(it, 1)
-        for phase in (up_owner, down_owner, down_core):
+        up_owner(it, 1)
+        for phase in (down_owner, down_core):
             for part in range(2):
                 phase(it, part)
         for part in range(2):
@@ -320,7 +322,7 @@
             compiler_params=pltpu.CompilerParams(
                 collective_id=0, has_side_effects=True, vmem_limit_bytes=VMEM_MIB * 1024 * 1024
             ),
-        )(step, mass, field)
+        )(step, mass, pltpu.with_memory_space_constraint(field, pltpu.HBM))
 
     return jax.shard_map(
         on_device,

time: 61.8 us -> 56.7 us (0.917)
  Pallas kernels: 57.5 us -> 54 us
  local copies, waits for them, and re-layouts: 2.91 us -> 1.32 us
    pallas_call x1, Pallas kernels: 57.5 us -> 54 us  [on_device(): pl.pallas_call(functools.partial(kernel, nz, ny, slices), out_shape=jax.S...]
    unnamed x3 -> x1, local copies, waits for them, and re-layouts: 2.91 us -> 1.32 us
where the time goes in v4:
time: 56.7 us; the launch traced here: 56.6 us
  Pallas kernels  54 us (95%)
  local copies, waits for them, and re-layouts  1.32 us (2%)
  between operations  1.3 us (2%)
    pallas_call x1, Pallas kernels, on_device(): pl.pallas_call(functools.partial(kernel, nz, ny, slices), out_shape=jax.S...  54 us
    unnamed x1, local copies, waits for them, and re-layouts  1.32 us

profile of v4, /device:TPU:1, one launch (start us, length us, event | category | flops | bytes accessed | tf_op | source)
XLA Modules:
  0.0 56.6 jit_solution(7512153911415846039)
XLA Ops:
  1.3 54.0 %shard_map.37 = f32[8,32,2048]{2,1,0:T(8,128)S(1)} custom-call(f32[1]{0:T(128)S(6)} %copy.5.step_ref, f32[1]{0:T(128)S(6)} %copy.6.mass_ref, f32[8,32,2048]{2,1,0:T(8,128)} %field.1), custom_call_target="tpu_custom_call" | custom-call | tf_op jit(solution)/shard_map/pallas_call | solution.py:294
  55.3 1.3 %copy.7 = f32[8,32,2048]{2,1,0:T(8,128)} copy(f32[8,32,2048]{2,1,0:T(8,128)S(1)} %shard_map.37) | data formatting | bytes 4194304

commit v5 on v4

--- a/solution.py
+++ b/solution.py
@@ -15,10 +15,10 @@
 MESH = pl.DeviceIdType.MESH
 
 
-def kernel(nz, ny, slices, step_ref, mass_ref, field, out, fb, gb, hs, hb, mom, u1, xs, zr, ws, wr, cs, yv,
+def kernel(nz, ny, slices, step_ref, mass_ref, field, out, fb, gb, hs, hb, hm, mom, u1, xs, zr, ws, wr, cs, yv,
            load_sem, send, recv, hsend, hrecv):
     tiles = fb.shape[1] - 2
-    groups = fb.shape[2] // ROWS
+    groups = fb.shape[2] // ROWS - 2
     tm, sp = lax.axis_index("tm"), lax.axis_index("space")
     z, h, c = tm // 4, (tm // 2) % 2, tm % 2
     lo, y = sp // ny, sp % ny
@@ -48,7 +48,9 @@
 
     loads = [
         pltpu.make_async_copy(
-            field.at[:, :, pl.ds(k * LANES, LANES)], fb.at[:, k + 1], load_sem.at[k]
+            field.at[:, :, pl.ds(k * LANES, LANES)],
+            fb.at[:, k + 1, pl.ds(ROWS, groups * ROWS), :],
+            load_sem.at[k],
         )
         for k in range(tiles)
     ]
@@ -58,10 +60,14 @@
     full = lambda value: jnp.full((ROWS, LANES), value, jnp.float32)
     blank = full(0.0)
 
-    for t in range(slices):
-        for i in range(groups):
-            fb[t, 0, pl.ds(i * ROWS, ROWS), :] = blank
-            fb[t, tiles + 1, pl.ds(i * ROWS, ROWS), :] = blank
+    @pl.loop(0, slices)
+    def _(t):
+        for k in (0, tiles + 1):
+            for i in range(groups):
+                fb[t, k, pl.ds((i + 1) * ROWS, ROWS), :] = blank
+        for k in range(tiles):
+            fb[t, k + 1, pl.ds(0, ROWS), :] = blank
+            fb[t, k + 1, pl.ds((groups + 1) * ROWS, ROWS), :] = blank
 
     def clear(which):
         for it in range(ITERS):
@@ -100,30 +106,28 @@
 
     parts = (tuple(range(1, groups - 1)), (0, groups - 1))
 
-    def stencil(it, part):
+    def stencil(it, part, lacks):
         @pl.loop(0, tiles // 4)
         def _(quad):
             for k in (quad * 4 + j for j in range(4)):
                 for half, i in enumerate(parts[part]):
-                    rows = pl.ds(i * ROWS, ROWS)
+                    rows = pl.ds((i + 1) * ROWS, ROWS)
                     gs = []
                     for t in range(slices):
                         f = fb[t, k + 1, rows, :]
-                        if i == 0:
-                            xm = jnp.where(top, hb[it, 0, t, pl.ds(k, 1), :], pltpu.roll(f, 1, 0))
-                        else:
-                            xm = fb[t, k + 1, pl.ds(i * ROWS - 1, ROWS), :]
-                        if i == groups - 1:
-                            xp = jnp.where(bottom, hb[it, 1, t, pl.ds(k, 1), :], pltpu.roll(f, ROWS - 1, 0))
-                        else:
-                            xp = fb[t, k + 1, pl.ds(i * ROWS + 1, ROWS), :]
+                        xm = fb[t, k + 1, pl.ds((i + 1) * ROWS - 1, ROWS), :]
+                        xp = fb[t, k + 1, pl.ds((i + 1) * ROWS + 1, ROWS), :]
+                        if lacks and half == 0:
+                            xm = jnp.where(top, 0.0, xm)
+                        if lacks and half == 1:
+                            xp = jnp.where(bottom, 0.0, xp)
                         yp = pltpu.roll(jnp.where(low, fb[t, k + 2, rows, :], f), LANES - NZ, 1)
                         ym = pltpu.roll(jnp.where(high, fb[t, k, rows, :], f), NZ, 1)
                         zp = pltpu.roll(jnp.where(at_first, 0.0, f), LANES - 1, 1)
                         zm = pltpu.roll(jnp.where(at_last, 0.0, f), 1, 1)
                         near = (xm + xp) + (yp + ym) + (zp + zm)
                         g = f * (linear + f * (0.25 * f - 0.9)) - near
-                        gb[t, k, rows, :] = g
+                        gb[t, k, pl.ds(i * ROWS, ROWS), :] = g
                         gs.append(g)
                     before, after = gs[0], gs[-1]
                     for t in range(1, slices):
@@ -132,31 +136,77 @@
                     mom[it, part, half, k, 0] = before
                     mom[it, part, half, k, 1] = after
 
+    edges = (top, bottom)
+
+    def mend_outer_sums(it):
+        for half in range(2):
+            for lo_k in range(0, tiles, ROWS):
+                band = pl.ds(lo_k, ROWS)
+                planes = [hb[it, half, t, band, :] for t in range(slices)]
+                before, after = planes[0], planes[-1]
+                for t in range(1, slices):
+                    before = r * before + planes[t]
+                    after = r * after + planes[slices - 1 - t]
+                hm[half, 0, band, :] = before
+                hm[half, 1, band, :] = after
+            for k in range(tiles):
+                for which in range(2):
+                    add = jnp.where(edges[half], hm[half, which, pl.ds(k, 1), :], 0.0)
+                    mom[it, 1, half, k, which] = mom[it, 1, half, k, which] - add
+
+    def mend_outer(it):
+        @pl.loop(0, slices)
+        def _(t):
+            for half, i in enumerate(parts[1]):
+                rows = pl.ds(i * ROWS, ROWS)
+                for k in range(tiles):
+                    add = jnp.where(edges[half], hb[it, half, t, pl.ds(k, 1), :], 0.0)
+                    gb[t, k, rows, :] = gb[t, k, rows, :] - add
+
+    def mend_inner(it):
+        @pl.loop(0, slices)
+        def _(t):
+            for half, i in enumerate(parts[0]):
+                rows = pl.ds(i * ROWS, ROWS)
+                for k in range(tiles):
+                    shifted = fb[t, k + 1, pl.ds((i + 1) * ROWS + 2 * half - 1, ROWS), :]
+                    gb[t, k, rows, :] = gb[t, k, rows, :] - jnp.where(edges[half], shifted, 0.0)
+
     def solve(it, part):
         @pl.loop(0, tiles // 4)
         def _(quad):
             for j in range(4):
                 k = quad * 4 + j
                 for half, i in enumerate(parts[part]):
-                    rows = pl.ds(i * ROWS, ROWS)
-                    gs = [gb[t, k, rows, :] for t in range(slices)]
+                    rows = pl.ds((i + 1) * ROWS, ROWS)
+                    gs = [gb[t, k, pl.ds(i * ROWS, ROWS), :] for t in range(slices)]
                     state = yv[it, part, half, k, 0]
                     states = []
                     for t in range(slices):
                         state = r * state + gs[t]
                         states.append(state)
                     ahead = r * yv[it, part, half, k, 1]
+                    news = [None] * slices
                     for t in reversed(range(slices)):
                         new = keep * fb[t, k + 1, rows, :] - gain * (states[t] + ahead)
+                        ahead = r * (gs[t] + ahead)
+                        news[t] = new
                         if it + 1 < ITERS:
                             fb[t, k + 1, rows, :] = new
                         else:
-                            out[t, rows, pl.ds(pl.multiple_of(k * LANES, LANES), LANES)] = new
-                        if it + 1 < ITERS and i == 0:
-                            hs[it + 1, 1, t, pl.ds(k, 1), :] = new[:1]
-                        if it + 1 < ITERS and i == groups - 1:
-                            hs[it + 1, 0, t, pl.ds(k, 1), :] = new[ROWS - 1 :]
-                        ahead = r * (gs[t] + ahead)
+                            out[t, pl.ds(i * ROWS, ROWS), pl.ds(pl.multiple_of(k * LANES, LANES), LANES)] = new
+                        if it + 1 < ITERS and part == 1:
+                            edge = half * (ROWS - 1)
+                            hs[it + 1, 1 - half, t, pl.ds(k, 1), :] = new[edge : edge + 1]
+                    if it + 1 < ITERS and part == 1:
+                        before, after = news[0], news[-1]
+                        for t in range(1, slices):
+                            before = r * before + news[t]
+                            after = r * after + news[slices - 1 - t]
+                        turn = (1, ROWS - 1)[half]
+                        for which, add in enumerate((before, after)):
+                            add = jnp.where(edges[half], pltpu.roll(add, turn, 0), 0.0)
+                            mom[it + 1, 0, half, k, which] = mom[it + 1, 0, half, k, which] - add
 
     pending = []
 
@@ -178,7 +228,7 @@
         def _(t):
             for which, edge in enumerate((groups * ROWS - 1, 0)):
                 for k in range(tiles):
-                    hs[it, which, t, pl.ds(k, 1), :] = fb[t, k + 1, pl.ds(edge, 1), :]
+                    hs[it, which, t, pl.ds(k, 1), :] = fb[t, k + 1, pl.ds(ROWS + edge, 1), :]
 
     def halo(it, which):
         return copy(
@@ -254,25 +304,31 @@
     for load in loads:
         load.wait()
     pack(0)
-    stencil(0, 0)
+    stencil(0, 0, False)
     pl.semaphore_wait(barrier, 2 * nz + 1 + has_left.astype(jnp.int32) + has_right.astype(jnp.int32))
     send_halo(0)
     for it in range(ITERS):
         up_core(it, 0)
+        stencil(it, 1, False)
         up_owner(it, 0)
         wait_halo(it)
-        stencil(it, 1)
+        mend_outer_sums(it)
         up_core(it, 1)
+        mend_outer(it)
+        if it > 0:
+            mend_inner(it)
         up_owner(it, 1)
         for phase in (down_owner, down_core):
             for part in range(2):
                 phase(it, part)
-        for part in range(2):
-            arrive(yv.at[it, part, 1 - c], it, part, back)
-            solve(it, part)
+        arrive(yv.at[it, 0, 1 - c], it, 0, back)
+        solve(it, 0)
+        if it + 1 < ITERS:
+            stencil(it + 1, 0, True)
+        arrive(yv.at[it, 1, 1 - c], it, 1, back)
+        solve(it, 1)
         if it + 1 < ITERS:
             send_halo(it + 1)
-            stencil(it + 1, 0)
     for one_copy in pending:
         one_copy.wait_send()
     for it in range(ITERS):
@@ -301,10 +357,11 @@
             ],
             out_specs=pl.BlockSpec(memory_space=pltpu.VMEM),
             scratch_shapes=[
-                vmem(slices, tiles + 2, planes, LANES),
+                vmem(slices, tiles + 2, planes + 2 * ROWS, LANES),
                 vmem(slices, tiles, planes, LANES),
                 vmem(ITERS, 2, slices, tiles, LANES),
                 vmem(ITERS, 2, slices, tiles, LANES),
+                vmem(2, 2, tiles, LANES),
                 vmem(*level, 2, tiles, 2, *tile),
                 vmem(*level, tiles, 2, *tile),
                 vmem(*level, tiles, 2, *tile),

time: 56.7 us -> 55.4 us (0.977)
  Pallas kernels: 54 us -> 52.6 us
    pallas_call x1, Pallas kernels: 54 us -> 52.6 us  [on_device(): pl.pallas_call(functools.partial(kernel, nz, ny, slices), out_shape=jax.S...]
where the time goes in v5:
time: 55.4 us; the launch traced here: 55.3 us
  Pallas kernels  52.6 us (95%)
  local copies, waits for them, and re-layouts  1.32 us (2%)
  between operations  1.3 us (2%)
    pallas_call x1, Pallas kernels, on_device(): pl.pallas_call(functools.partial(kernel, nz, ny, slices), out_shape=jax.S...  52.6 us
    unnamed x1, local copies, waits for them, and re-layouts  1.32 us

profile of v5, /device:TPU:1, one launch (start us, length us, event | category | flops | bytes accessed | tf_op | source)
XLA Modules:
  0.0 55.3 jit_solution(12920244705596861307)
XLA Ops:
  1.3 52.6 %shard_map.37 = f32[8,32,2048]{2,1,0:T(8,128)S(1)} custom-call(f32[1]{0:T(128)S(6)} %copy.5.step_ref, f32[1]{0:T(128)S(6)} %copy.6.mass_ref, f32[8,32,2048]{2,1,0:T(8,128)} %field.1), custom_call_target="tpu_custom_call" | custom-call | tf_op jit(solution)/shard_map/pallas_call | solution.py:350
  53.9 1.3 %copy.7 = f32[8,32,2048]{2,1,0:T(8,128)} copy(f32[8,32,2048]{2,1,0:T(8,128)S(1)} %shard_map.37) | data formatting | bytes 4194304

commit v6 on v5

--- a/solution.py
+++ b/solution.py
@@ -15,7 +15,7 @@
 MESH = pl.DeviceIdType.MESH
 
 
-def kernel(nz, ny, slices, step_ref, mass_ref, field, out, fb, gb, hs, hb, hm, mom, u1, xs, zr, ws, wr, cs, yv,
+def kernel(nz, ny, slices, step_ref, mass_ref, field, out, fb, gb, hs, hb, hq, hm, mom, u1, xs, zr, ws, wr, cs, yv,
            load_sem, send, recv, hsend, hrecv):
     tiles = fb.shape[1] - 2
     groups = fb.shape[2] // ROWS - 2
@@ -72,6 +72,7 @@
     def clear(which):
         for it in range(ITERS):
             hb[it, which] = jnp.zeros(hb.shape[2:], jnp.float32)
+            hm[it, which] = jnp.zeros(hm.shape[2:], jnp.float32)
 
     pl.when(jnp.logical_not(has_left))(lambda: clear(0))
     pl.when(jnp.logical_not(has_right))(lambda: clear(1))
@@ -138,20 +139,23 @@
 
     edges = (top, bottom)
 
-    def mend_outer_sums(it):
-        for half in range(2):
+    def edge_sums(it):
+        for side in range(2):
             for lo_k in range(0, tiles, ROWS):
                 band = pl.ds(lo_k, ROWS)
-                planes = [hb[it, half, t, band, :] for t in range(slices)]
+                planes = [hs[it, side, t, band, :] for t in range(slices)]
                 before, after = planes[0], planes[-1]
                 for t in range(1, slices):
                     before = r * before + planes[t]
                     after = r * after + planes[slices - 1 - t]
-                hm[half, 0, band, :] = before
-                hm[half, 1, band, :] = after
+                hq[it, side, 0, band, :] = before
+                hq[it, side, 1, band, :] = after
+
+    def mend_outer_sums(it):
+        for half in range(2):
             for k in range(tiles):
                 for which in range(2):
-                    add = jnp.where(edges[half], hm[half, which, pl.ds(k, 1), :], 0.0)
+                    add = jnp.where(edges[half], hm[it, half, which, pl.ds(k, 1), :], 0.0)
                     mom[it, 1, half, k, which] = mom[it, 1, half, k, which] - add
 
     def mend_outer(it):
@@ -172,12 +176,13 @@
                     shifted = fb[t, k + 1, pl.ds((i + 1) * ROWS + 2 * half - 1, ROWS), :]
                     gb[t, k, rows, :] = gb[t, k, rows, :] - jnp.where(edges[half], shifted, 0.0)
 
-    def solve(it, part):
+    def solve(it, part, halves):
         @pl.loop(0, tiles // 4)
         def _(quad):
             for j in range(4):
                 k = quad * 4 + j
-                for half, i in enumerate(parts[part]):
+                for half in halves:
+                    i = parts[part][half]
                     rows = pl.ds((i + 1) * ROWS, ROWS)
                     gs = [gb[t, k, pl.ds(i * ROWS, ROWS), :] for t in range(slices)]
                     state = yv[it, part, half, k, 0]
@@ -203,8 +208,9 @@
                         for t in range(1, slices):
                             before = r * before + news[t]
                             after = r * after + news[slices - 1 - t]
-                        turn = (1, ROWS - 1)[half]
+                        turn, at = (1, ROWS - 1)[half], half * (ROWS - 1)
                         for which, add in enumerate((before, after)):
+                            hq[it + 1, 1 - half, which, pl.ds(k, 1), :] = add[at : at + 1]
                             add = jnp.where(edges[half], pltpu.roll(add, turn, 0), 0.0)
                             mom[it + 1, 0, half, k, which] = mom[it + 1, 0, half, k, which] - add
 
@@ -230,22 +236,23 @@
                 for k in range(tiles):
                     hs[it, which, t, pl.ds(k, 1), :] = fb[t, k + 1, pl.ds(ROWS + edge, 1), :]
 
-    def halo(it, which):
+    def halo(it, which, kind):
+        src, dst = ((hq, hm), (hs, hb))[kind]
         return copy(
-            hs.at[it, which],
-            hb.at[it, which],
-            hsend.at[it, which],
-            hrecv.at[it, which],
+            src.at[it, which],
+            dst.at[it, which],
+            hsend.at[it, which, kind],
+            hrecv.at[it, which, kind],
             (tm, sp + 1) if which == 0 else (tm, sp - 1),
         )
 
-    def send_halo(it):
-        pl.when(has_right)(lambda: halo(it, 0).start())
-        pl.when(has_left)(lambda: halo(it, 1).start())
-
-    def wait_halo(it):
-        pl.when(has_left)(lambda: halo(it, 0).wait_recv())
-        pl.when(has_right)(lambda: halo(it, 1).wait_recv())
+    def send_halo(it, kind):
+        pl.when(has_right)(lambda: halo(it, 0, kind).start())
+        pl.when(has_left)(lambda: halo(it, 1, kind).start())
+
+    def wait_halo(it, kind):
+        pl.when(has_left)(lambda: halo(it, 0, kind).wait_recv())
+        pl.when(has_right)(lambda: halo(it, 1, kind).wait_recv())
 
     up = lambda d, hd: 1 + 2 * d + hd
     down = lambda d, hd: 1 + 2 * nz + 2 * d + hd
@@ -304,36 +311,45 @@
     for load in loads:
         load.wait()
     pack(0)
+    edge_sums(0)
     stencil(0, 0, False)
     pl.semaphore_wait(barrier, 2 * nz + 1 + has_left.astype(jnp.int32) + has_right.astype(jnp.int32))
-    send_halo(0)
+    send_halo(0, 0)
+    send_halo(0, 1)
     for it in range(ITERS):
         up_core(it, 0)
         stencil(it, 1, False)
         up_owner(it, 0)
-        wait_halo(it)
+        wait_halo(it, 0)
         mend_outer_sums(it)
         up_core(it, 1)
-        mend_outer(it)
         if it > 0:
             mend_inner(it)
         up_owner(it, 1)
-        for phase in (down_owner, down_core):
-            for part in range(2):
-                phase(it, part)
+        wait_halo(it, 1)
+        mend_outer(it)
+        down_owner(it, 0)
+        down_owner(it, 1)
+        down_core(it, 0)
         arrive(yv.at[it, 0, 1 - c], it, 0, back)
-        solve(it, 0)
+        solve(it, 0, (0, 1))
         if it + 1 < ITERS:
             stencil(it + 1, 0, True)
-        arrive(yv.at[it, 1, 1 - c], it, 1, back)
-        solve(it, 1)
+        down_core(it, 1)
+        for own in (True, False):
+            if not own:
+                arrive(yv.at[it, 1, 1 - c], it, 1, back)
+            pl.when(first == own)(lambda: solve(it, 1, (0,)))
+            pl.when(first != own)(lambda: solve(it, 1, (1,)))
         if it + 1 < ITERS:
-            send_halo(it + 1)
+            send_halo(it + 1, 0)
+            send_halo(it + 1, 1)
     for one_copy in pending:
         one_copy.wait_send()
     for it in range(ITERS):
-        pl.when(has_right)(lambda: halo(it, 0).wait_send())
-        pl.when(has_left)(lambda: halo(it, 1).wait_send())
+        for kind in range(2):
+            pl.when(has_right)(lambda: halo(it, 0, kind).wait_send())
+            pl.when(has_left)(lambda: halo(it, 1, kind).wait_send())
 
 
 def solution(mesh):
@@ -361,7 +377,8 @@
                 vmem(slices, tiles, planes, LANES),
                 vmem(ITERS, 2, slices, tiles, LANES),
                 vmem(ITERS, 2, slices, tiles, LANES),
-                vmem(2, 2, tiles, LANES),
+                vmem(ITERS, 2, 2, tiles, LANES),
+                vmem(ITERS, 2, 2, tiles, LANES),
                 vmem(*level, 2, tiles, 2, *tile),
                 vmem(*level, tiles, 2, *tile),
                 vmem(*level, tiles, 2, *tile),
@@ -373,8 +390,8 @@
                 pltpu.SemaphoreType.DMA((tiles,)),
                 pltpu.SemaphoreType.DMA((*level, sems)),
                 pltpu.SemaphoreType.DMA((*level, sems)),
-                pltpu.SemaphoreType.DMA((ITERS, 2)),
-                pltpu.SemaphoreType.DMA((ITERS, 2)),
+                pltpu.SemaphoreType.DMA((ITERS, 2, 2)),
+                pltpu.SemaphoreType.DMA((ITERS, 2, 2)),
             ],
             compiler_params=pltpu.CompilerParams(
                 collective_id=0, has_side_effects=True, vmem_limit_bytes=VMEM_MIB * 1024 * 1024

time: 55.4 us -> 54.3 us (0.980)
  Pallas kernels: 52.6 us -> 51.6 us
    pallas_call x1, Pallas kernels: 52.6 us -> 51.6 us  [on_device(): pl.pallas_call(functools.partial(kernel, nz, ny, slices), out_shape=jax.S...]
where the time goes in v6:
time: 54.3 us; the launch traced here: 54.2 us
  Pallas kernels  51.6 us (95%)
  local copies, waits for them, and re-layouts  1.32 us (2%)
  between operations  1.3 us (2%)
    pallas_call x1, Pallas kernels, on_device(): pl.pallas_call(functools.partial(kernel, nz, ny, slices), out_shape=jax.S...  51.6 us
    unnamed x1, local copies, waits for them, and re-layouts  1.32 us

profile of v6, /device:TPU:1, one launch (start us, length us, event | category | flops | bytes accessed | tf_op | source)
XLA Modules:
  0.0 54.2 jit_solution(17954540141006704419)
XLA Ops:
  1.3 51.6 %shard_map.37 = f32[8,32,2048]{2,1,0:T(8,128)S(1)} custom-call(f32[1]{0:T(128)S(6)} %copy.5.step_ref, f32[1]{0:T(128)S(6)} %copy.6.mass_ref, f32[8,32,2048]{2,1,0:T(8,128)} %field.1), custom_call_target="tpu_custom_call" | custom-call | tf_op jit(solution)/shard_map/pallas_call | solution.py:366
  52.9 1.3 %copy.7 = f32[8,32,2048]{2,1,0:T(8,128)} copy(f32[8,32,2048]{2,1,0:T(8,128)S(1)} %shard_map.37) | data formatting | bytes 4194304

commit v7 on v6

--- a/solution.py
+++ b/solution.py
@@ -16,7 +16,7 @@
 
 
 def kernel(nz, ny, slices, step_ref, mass_ref, field, out, fb, gb, hs, hb, hq, hm, mom, u1, xs, zr, ws, wr, cs, yv,
-           load_sem, send, recv, hsend, hrecv):
+           load_sem, send, recv, hsend, hrecv, qsend, qrecv):
     tiles = fb.shape[1] - 2
     groups = fb.shape[2] // ROWS - 2
     tm, sp = lax.axis_index("tm"), lax.axis_index("space")
@@ -37,6 +37,8 @@
         for hd in range(2):
             greet(owner(d, hd))
     greet(other)
+    has_mine = jnp.where(c == 0, has_left, has_right)
+    pl.when(has_mine)(lambda: greet((tm + 1 - 2 * c, sp - 1 + 2 * c)))
 
     @pl.when(has_left)
     def _():
@@ -72,7 +74,10 @@
     def clear(which):
         for it in range(ITERS):
             hb[it, which] = jnp.zeros(hb.shape[2:], jnp.float32)
-            hm[it, which] = jnp.zeros(hm.shape[2:], jnp.float32)
+
+    @pl.when(jnp.logical_not(has_mine))
+    def _():
+        hm[...] = jnp.zeros(hm.shape, jnp.float32)
 
     pl.when(jnp.logical_not(has_left))(lambda: clear(0))
     pl.when(jnp.logical_not(has_right))(lambda: clear(1))
@@ -138,6 +143,7 @@
                     mom[it, part, half, k, 1] = after
 
     edges = (top, bottom)
+    edge = row == c * (ROWS - 1)
 
     def edge_sums(it):
         for side in range(2):
@@ -152,11 +158,13 @@
                 hq[it, side, 1, band, :] = after
 
     def mend_outer_sums(it):
-        for half in range(2):
-            for k in range(tiles):
-                for which in range(2):
-                    add = jnp.where(edges[half], hm[it, half, which, pl.ds(k, 1), :], 0.0)
-                    mom[it, 1, half, k, which] = mom[it, 1, half, k, which] - add
+        for k in range(tiles):
+            line = pl.ds(k, 1)
+            for which in range(2):
+                own = jnp.where(edge, hm[it, c, which, line, :], 0.0)
+                theirs = jnp.where(edge, hm[it, 1 - c, which, line, :], 0.0)
+                mom[it, 1, c, k, which] = mom[it, 1, c, k, which] - own
+                u1[it, 1, k, which] = u1[it, 1, k, which] - theirs
 
     def mend_outer(it):
         @pl.loop(0, slices)
@@ -236,23 +244,37 @@
                 for k in range(tiles):
                     hs[it, which, t, pl.ds(k, 1), :] = fb[t, k + 1, pl.ds(ROWS + edge, 1), :]
 
-    def halo(it, which, kind):
-        src, dst = ((hq, hm), (hs, hb))[kind]
+    def halo(it, which):
         return copy(
-            src.at[it, which],
-            dst.at[it, which],
-            hsend.at[it, which, kind],
-            hrecv.at[it, which, kind],
+            hs.at[it, which],
+            hb.at[it, which],
+            hsend.at[it, which],
+            hrecv.at[it, which],
             (tm, sp + 1) if which == 0 else (tm, sp - 1),
         )
 
-    def send_halo(it, kind):
-        pl.when(has_right)(lambda: halo(it, 0, kind).start())
-        pl.when(has_left)(lambda: halo(it, 1, kind).start())
-
-    def wait_halo(it, kind):
-        pl.when(has_left)(lambda: halo(it, 0, kind).wait_recv())
-        pl.when(has_right)(lambda: halo(it, 1, kind).wait_recv())
+    def halo_sums(it, which, source):
+        return copy(
+            hq.at[it, which],
+            hm.at[it, source],
+            qsend.at[it, which],
+            qrecv.at[it, source],
+            (tm - c + which, sp + 1 - 2 * which),
+        )
+
+    def send_halo(it):
+        pl.when(has_right)(lambda: halo_sums(it, 0, c).start())
+        pl.when(has_left)(lambda: halo_sums(it, 1, c).start())
+        pl.when(has_right)(lambda: halo(it, 0).start())
+        pl.when(has_left)(lambda: halo(it, 1).start())
+
+    def wait_sums(it):
+        for source in range(2):
+            pl.when(has_mine)(lambda: halo_sums(it, 0, source).wait_recv())
+
+    def wait_halo(it):
+        pl.when(has_left)(lambda: halo(it, 0).wait_recv())
+        pl.when(has_right)(lambda: halo(it, 1).wait_recv())
 
     up = lambda d, hd: 1 + 2 * d + hd
     down = lambda d, hd: 1 + 2 * nz + 2 * d + hd
@@ -263,6 +285,9 @@
 
     def up_owner(it, part):
         arrive(u1.at[it, part], it, part, 0)
+        if part == 1:
+            wait_sums(it)
+            mend_outer_sums(it)
         for k in range(tiles):
             xs[it, part, k, 0] = wa * mom[it, part, c, k, 0] + wb * u1[it, part, k, 0]
             xs[it, part, k, 1] = wb * mom[it, part, c, k, 1] + wa * u1[it, part, k, 1]
@@ -313,20 +338,17 @@
     pack(0)
     edge_sums(0)
     stencil(0, 0, False)
-    pl.semaphore_wait(barrier, 2 * nz + 1 + has_left.astype(jnp.int32) + has_right.astype(jnp.int32))
-    send_halo(0, 0)
-    send_halo(0, 1)
+    pl.semaphore_wait(barrier, 2 * nz + 1 + has_left.astype(jnp.int32) + has_right.astype(jnp.int32) + has_mine.astype(jnp.int32))
+    send_halo(0)
     for it in range(ITERS):
         up_core(it, 0)
         stencil(it, 1, False)
+        up_core(it, 1)
         up_owner(it, 0)
-        wait_halo(it, 0)
-        mend_outer_sums(it)
-        up_core(it, 1)
         if it > 0:
             mend_inner(it)
         up_owner(it, 1)
-        wait_halo(it, 1)
+        wait_halo(it)
         mend_outer(it)
         down_owner(it, 0)
         down_owner(it, 1)
@@ -342,14 +364,13 @@
             pl.when(first == own)(lambda: solve(it, 1, (0,)))
             pl.when(first != own)(lambda: solve(it, 1, (1,)))
         if it + 1 < ITERS:
-            send_halo(it + 1, 0)
-            send_halo(it + 1, 1)
+            send_halo(it + 1)
     for one_copy in pending:
         one_copy.wait_send()
     for it in range(ITERS):
-        for kind in range(2):
-            pl.when(has_right)(lambda: halo(it, 0, kind).wait_send())
-            pl.when(has_left)(lambda: halo(it, 1, kind).wait_send())
+        for kind in (halo, lambda it, which: halo_sums(it, which, c)):
+            pl.when(has_right)(lambda: kind(it, 0).wait_send())
+            pl.when(has_left)(lambda: kind(it, 1).wait_send())
 
 
 def solution(mesh):
@@ -390,8 +411,10 @@
                 pltpu.SemaphoreType.DMA((tiles,)),
                 pltpu.SemaphoreType.DMA((*level, sems)),
                 pltpu.SemaphoreType.DMA((*level, sems)),
-                pltpu.SemaphoreType.DMA((ITERS, 2, 2)),
-                pltpu.SemaphoreType.DMA((ITERS, 2, 2)),
+                pltpu.SemaphoreType.DMA((ITERS, 2)),
+                pltpu.SemaphoreType.DMA((ITERS, 2)),
+                pltpu.SemaphoreType.DMA((ITERS, 2)),
+                pltpu.SemaphoreType.DMA((ITERS, 2)),
             ],
             compiler_params=pltpu.CompilerParams(
                 collective_id=0, has_side_effects=True, vmem_limit_bytes=VMEM_MIB * 1024 * 1024

time: 54.3 us -> 54 us (level)
  no operation moved by 1% of the time
where the time goes in v7:
time: 54 us; the launch traced here: 53.8 us
  Pallas kernels  51.2 us (95%)
  local copies, waits for them, and re-layouts  1.32 us (2%)
  between operations  1.3 us (2%)
    pallas_call x1, Pallas kernels, on_device(): pl.pallas_call(functools.partial(kernel, nz, ny, slices), out_shape=jax.S...  51.2 us
    unnamed x1, local copies, waits for them, and re-layouts  1.32 us

profile of v7, /device:TPU:1, one launch (start us, length us, event | category | flops | bytes accessed | tf_op | source)
XLA Modules:
  0.0 53.8 jit_solution(10824400175880022745)
XLA Ops:
  1.3 51.2 %shard_map.37 = f32[8,32,2048]{2,1,0:T(8,128)S(1)} custom-call(f32[1]{0:T(128)S(6)} %copy.5.step_ref, f32[1]{0:T(128)S(6)} %copy.6.mass_ref, f32[8,32,2048]{2,1,0:T(8,128)} %field.1), custom_call_target="tpu_custom_call" | custom-call | tf_op jit(solution)/shard_map/pallas_call | solution.py:387
  52.5 1.3 %copy.7 = f32[8,32,2048]{2,1,0:T(8,128)} copy(f32[8,32,2048]{2,1,0:T(8,128)S(1)} %shard_map.37) | data formatting | bytes 4194304
